TPU v7x, 128 devices: a whole 4x4x4 slice. The times are simulated.
128 devices in a mesh: mb: 4 (over y), feat: 32 (over z, x, core).
Axes of the slice: x: 4, y: 4, z: 4, core: 2. Of those that a mesh axis runs over, the one named last changes fastest.
Arguments:
- features: float32 [1024, 262144], P('feat', 'mb'), may hold values from -6 to 6
- tile_rows: int32 [768], P('mb'), may hold values from 0 to 127
- tile_cols: int32 [768], P('mb'), may hold values from 0 to 511
- tile_masks: int32 [768, 128, 128], P('mb'), may hold values 0 or 1
- weight: bfloat16 [1024, 256], replicated, may hold values from -0.5625 to 0.5625
- upstream: bfloat16 [65536, 256], P(('mb', 'feat')), may hold values from -6 to 6
Outputs:
- activation: bfloat16 [65536, 256], P(('mb', 'feat'))
- weight_grad: float32 [1024, 256], P('feat')
All inputs are finite; a program needn't handle non-finite values. No bound on the sum of `tile_masks` on one device may be relied on, other than what follows from the above.
Results may differ from a plain program's by a relative error of at most 0.0063.
Values may be sent and summed in bfloat16 or wider, within the bound.
No kernel may reach another device: no remote copies, remote signals or barrier semaphores. Data moves between devices by JAX's collectives and lax.ppermute only.
A program may use at most 128 MiB of HBM per device.

v0:
```python
import jax
import jax.numpy as jnp
from jax import lax
from jax.sharding import PartitionSpec as P

NT = 16384


def smooth_gate(values):
    return 0.5 * values * (1.0 + lax.erf(values * 0.7071067811865476))


def gate_slope(values):
    return (
        0.5 * (1.0 + lax.erf(values * 0.7071067811865476))
        + values * jnp.exp(-0.5 * values * values) * 0.3989422804014327
    )


def neighbor_mean(sources, row_index, col_index, masks):
    feat_cols = sources.shape[0]
    src_count = sources.shape[1]
    tile_size = masks.shape[1]
    row_tiles = NT // tile_size
    blocks = sources.reshape(feat_cols, src_count // tile_size, tile_size)
    picked = jnp.take(blocks, col_index, axis=1)
    weights = masks.astype(jnp.float32)
    contrib = jnp.einsum("fts,tds->tfd", picked, weights, precision=lax.Precision.HIGHEST)
    onehot = (row_index[None, :] == jnp.arange(row_tiles, dtype=jnp.int32)[:, None]).astype(
        jnp.float32
    )
    summed = jnp.einsum("rt,tfd->frd", onehot, contrib, precision=lax.Precision.HIGHEST).reshape(
        feat_cols, NT
    )
    degree = jnp.dot(onehot, jnp.sum(weights, axis=2), precision=lax.Precision.HIGHEST).reshape(NT)
    return ((sources[:, :NT] + summed) / (degree[None, :] + 1.0)).astype(jnp.bfloat16)


def per_device(features, tile_rows, tile_cols, tile_masks, weight, upstream):
    hidden_t = neighbor_mean(features, tile_rows, tile_cols, tile_masks)
    feat_cols = hidden_t.shape[0]
    weight_part = lax.dynamic_slice_in_dim(weight, lax.axis_index("feat") * feat_cols, feat_cols, 0)
    picked = hidden_t
    preact = lax.psum_scatter(
        lax.dot_general(
            picked, weight_part, (((0,), (0,)), ((), ())), preferred_element_type=jnp.float32
        ),
        "feat",
        scatter_dimension=0,
        tiled=True,
    )
    slopes = (upstream.astype(jnp.float32) * gate_slope(preact)).astype(jnp.bfloat16)
    picked = hidden_t
    local_grad = jnp.dot(
        picked,
        lax.all_gather(slopes, "feat", axis=0, tiled=True),
        preferred_element_type=jnp.float32,
    )
    activation = smooth_gate(preact).astype(jnp.bfloat16)
    weight_grad = lax.psum(local_grad, "mb")
    return (activation, weight_grad)


def solution(mesh):
    return jax.shard_map(
        per_device,
        mesh=mesh,
        in_specs=(
            P("feat", "mb"),
            P("mb"),
            P("mb"),
            P("mb", None, None),
            P(),
            P(("mb", "feat"), None),
        ),
        out_specs=(P(("mb", "feat"), None), P("feat", None)),
        check_vma=False,
    )
```

profile of v0, /device:TPU:0, one launch (start us, length us, event | category | flops | bytes accessed | tf_op | source)
XLA Modules:
  0.0 273.4 jit_solution(18257796936870843259)
XLA Ops:
  7.2 0.0 copy-start
  7.2 0.0 reduce-scatter.2.cloned.1.call-start
  7.2 0.7 compare_and_fusion
  8.0 0.7 compare_select_fusion
  8.7 7.9 %convert_reduce_fusion = f32[192,128]{1,0:T(8,128)S(1)} fusion(s32[192,128,128]{2,1,0:T(8,128)} %param.9), kind=kLoop, calls=%fused_computation.1 | loop fusion | flops 6266880 | bytes 12681216 | tf_op jit(solution)/shard_map/reduce_sum | solution.py:35
  16.5 0.0 copy-start.3
  16.6 7.8 %copy_bitcast_fusion = f32[32,512,128]{2,0,1:T(8,128)} fusion(f32[32,65536]{1,0:T(8,128)} %param.6), kind=kLoop, calls=%fused_computation.4 | loop fusion | bytes 16777216 | tf_op jit(solution)/shard_map/reshape | solution.py:25
  24.4 0.0 copy-done.3
  24.4 0.4 fusion.13
  24.8 5.9 %gather_fusion = f32[192,32,128]{2,1,0:T(8,128)} fusion(f32[32,512,128]{2,0,1:T(8,128)} %copy_bitcast_fusion, s32[1024]{0:T(1024)S(1)} %pad_clamp_fusion), kind=kCustom, calls=%fused_computation | custom fusion | bytes 6292224 | tf_op jit(solution)/shard_map/jit(_take)/gather | solution.py:26
  30.6 22.4 %fusion = f32[192,32,128]{2,1,0:T(8,128)S(1)} fusion(s32[192,128,128]{2,1,0:T(8,128)} %param.9, f32[192,32,128]{2,1,0:T(8,128)} %gather_fusion, pred[192]{0:T(512)(128)(4,1)S(1)} %compare_and_fusion), kind=kOutput, calls=%fused_computation.2 | convolution fusion | flops 1211891712 | bytes 18874560 | tf_op jit(solution)/shard_map/fts,tds->tfd/dot_general | solution.py:28
  53.1 4.7 %fusion.8 = f32[32,128,128]{1,2,0:T(8,128)S(1)} fusion(f32[192,32,128]{2,1,0:T(8,128)S(1)} %fusion, s32[192]{0:T(256)S(1)} %copy-done.3), kind=kOutput, calls=%fused_computation.12 | convolution fusion | flops 1207984128 | bytes 5243648 | tf_op jit(solution)/shard_map/rt,tfd->frd/dot_general | solution.py:32
  57.8 1.9 copy.11
  59.6 3.5 %fusion.7 = bf16[32,16384]{1,0:T(8,128)(2,1)S(1)} fusion(f32[4,8,128,128]{3,2,1,0:T(8,128)} %bitcast.26, f32[32,65536]{1,0:T(8,128)} %param.6, f32[16384]{0:T(1024)S(1)} %fusion.13), kind=kLoop, calls=%fused_computation.11 | loop fusion | flops 1572864 | bytes 5308416 | tf_op jit(solution)/shard_map/convert_element_type | solution.py:36
  63.1 0.0 copy-done
  63.1 8.1 %fusion.24 = f32[16384,256]{1,0:T(8,128)} fusion(bf16[32,16384]{1,0:T(8,128)(2,1)S(1)} %fusion.7, bf16[1024,256]{1,0:T(8,128)(2,1)S(1)} %copy-done, s32[]{:T(128)S(6)} %select_n.14), kind=kOutput, calls=%fused_computation.30 | convolution fusion | flops 268435456 | bytes 17842180 | tf_op jit(solution)/shard_map/dot_general | solution.py:45
  71.2 0.0 copy-start.2
  71.2 0.0 reduce-scatter.2.cloned.1.call-update
  71.3 0.0 all-gather.2.cloned.1.call-start
  71.3 118.2 %reduce-scatter.2.cloned.1.call-done = f32[512,256]{1,0:T(8,128)} async-done(((f32[16384,256]{1,0:T(8,128)}), f32[512,256]{1,0:T(8,128)}) %reduce-scatter.2.cloned.1.call-update) | async-done | bytes 524304 | tf_op jit(solution)/shard_map/reduce_scatter | solution.py:44
  189.5 0.0 copy-done.2
  189.5 2.1 fusion.19
  191.7 0.0 all-gather.2.cloned.1.call-update
  191.7 52.2 %all-gather.2.cloned.1.call-done = bf16[16384,256]{1,0:T(8,128)(2,1)} async-done(((bf16[512,256]{1,0:T(8,128)(2,1)}), bf16[16384,256]{1,0:T(8,128)(2,1)}) %all-gather.2.cloned.1.call-update) | async-done | bytes 8388624 | tf_op jit(solution)/shard_map/all_gather | solution.py:56
  243.9 0.0 copy-start.1
  243.9 5.0 %fusion.28 = f32[32,256]{1,0:T(8,128)S(1)} fusion(bf16[32,16384]{1,0:T(8,128)(2,1)S(1)} %fusion.7, bf16[16384,256]{1,0:T(8,128)(2,1)} %all-gather.2.cloned.1.call-done), kind=kOutput, calls=%fused_computation.37 | convolution fusion | flops 268435456 | bytes 9469952 | tf_op jit(solution)/shard_map/dot_general | solution.py:54
  248.9 17.6 %psum.7 = f32[32,256]{1,0:T(8,128)} all-reduce(f32[32,256]{1,0:T(8,128)S(1)} %fusion.28), channel_id=1, replica_groups=mesh['mb'=4,'feat'=32] {'mb'}, use_global_device_ids=true, to_apply=%region_2.3 | all-reduce | flops 8192 | bytes 65536 | tf_op jit(solution)/shard_map/psum | solution.py:60
  266.5 0.0 copy-done.1
  (1 shorter events, 0.0 us)
Async XLA Ops:
  7.2 55.9 %copy-start = (bf16[1024,256]{1,0:T(8,128)(2,1)S(1)}, bf16[1024,256]{1,0:T(8,128)(2,1)}, u32[]{:S(2)}) copy-start(bf16[1024,256]{1,0:T(8,128)(2,1)} %param.10) | copy-start | bytes 1572868
  7.2 182.4 %reduce-scatter.2.cloned.1.call-start = ((), (), s32[]{:S(2)}) async-start(), calls=%async_computation.1 | async-start | bytes 17301504 | tf_op jit(solution)/shard_map/reduce_scatter | solution.py:44
  16.5 7.8 %copy-start.3 = (s32[192]{0:T(256)S(1)}, s32[192]{0:T(256)}, u32[]{:S(2)}) copy-start(s32[192]{0:T(256)} %param.7) | copy-start | bytes 2308
  71.2 118.3 %copy-start.2 = (bf16[512,256]{1,0:T(8,128)(2,1)S(1)}, bf16[512,256]{1,0:T(8,128)(2,1)}, u32[]{:S(2)}) copy-start(bf16[512,256]{1,0:T(8,128)(2,1)} %param.11) | copy-start | bytes 786436
  71.3 172.7 %all-gather.2.cloned.1.call-start = ((), (), s32[]{:S(2)}) async-start(), calls=%async_computation.2 | async-start | bytes 8650752 | tf_op jit(solution)/shard_map/all_gather | solution.py:56
  243.9 22.6 %copy-start.1 = (bf16[1024,256]{1,0:T(8,128)(2,1)S(1)}, bf16[1024,256]{1,0:T(8,128)(2,1)}, u32[]{:S(2)}) copy-start(bf16[1024,256]{1,0:T(8,128)(2,1)} %param.10) | copy-start | bytes 1572868
Sparse Core Ops, SparseCore 0:
  71.4 118.1 reduce-scatter.1
  191.8 52.0 all-gather.1
where the time goes:
time: 274 us; the launch traced here: 273 us
  waiting for transfers between devices  170 us (62%)
  matrix products  40.6 us (15%)
  blocking collectives  17.6 us (6%)
  local copies, waits for them, and re-layouts  15.6 us (6%)
  other arithmetic  14.9 us (5%)
  between operations  14.1 us (5%)
    reduce_scatter x1, waiting for transfers between devices, per_device(): lax.psum_scatter(lax.dot_general(picked, weight_part, (((0,), (0,)), ((),...  118 us
    all_gather x1, waiting for transfers between devices, per_device(): lax.all_gather(slopes, 'feat', axis=0, tiled=True)  52.2 us
    dot_general x1, matrix products, neighbor_mean(): jnp.einsum('fts,tds->tfd', picked, weights, precision=lax.Precision.HIGHEST)  22.4 us
    psum x1, blocking collectives, per_device(): weight_grad = lax.psum(local_grad, 'mb')  17.6 us
    dot_general x1, matrix products, per_device(): lax.dot_general(picked, weight_part, (((0,), (0,)), ((), ())), preferred_...  8.13 us
    reduce_sum x1, other arithmetic, neighbor_mean(): jnp.sum(weights, axis=2)  7.89 us
    reshape x1, local copies, waits for them, and re-layouts, neighbor_mean(): blocks = sources.reshape(feat_cols, src_count // tile_size, tile_size)  7.81 us
    gather x1, local copies, waits for them, and re-layouts, neighbor_mean(): picked = jnp.take(blocks, col_index, axis=1)  5.89 us
  transfers between devices with their start and end apart: 2, of which 2 were waited for; matrix products, arithmetic and copies ran while one was open for 0% of the time, Pallas kernels for 0%

commit v1 on v0

v1 whole, which is shorter than its diff:
```python
import jax
import jax.numpy as jnp
from jax import lax
from jax.experimental import pallas as pl
from jax.experimental.pallas import tpu as pltpu
from jax.sharding import PartitionSpec as P

NT = 16384
TILE = 128
CHUNK = 16
AHEAD = 4


def aggregate_kernel(
    row_index,
    col_index,
    features,
    masks,
    hidden,
    rows,
    cols,
    total,
    degree,
    picked,
    mask_buf,
    index_sem,
    self_sem,
    pick_sem,
    mask_sem,
):
    feat_cols = features.shape[0]
    chunks = mask_buf.shape[0] // CHUNK
    peers, _, block = hidden.shape

    def mask_copy(chunk):
        span = pl.ds(chunk * CHUNK, CHUNK)
        return pltpu.make_async_copy(masks.at[span], mask_buf.at[span], mask_sem.at[chunk])

    def start_picks(chunk):
        for k in range(CHUNK):
            tile = chunk * CHUNK + k
            first = pl.multiple_of(cols[tile] * TILE, TILE)
            pltpu.make_async_copy(
                features.at[:, pl.ds(first, TILE)], picked.at[tile], pick_sem.at[chunk]
            ).start()

    fetch_rows = pltpu.make_async_copy(row_index, rows, index_sem.at[0])
    fetch_cols = pltpu.make_async_copy(col_index, cols, index_sem.at[1])
    own = pltpu.make_async_copy(features.at[:, pl.ds(0, NT)], total, self_sem)
    fetch_cols.start()
    fetch_rows.start()
    mask_copy(0).start()
    own.start()
    for chunk in range(1, AHEAD):
        mask_copy(chunk).start()
    fetch_cols.wait()
    for chunk in range(AHEAD):
        start_picks(chunk)
    fetch_rows.wait()
    degree[...] = jnp.zeros_like(degree)
    own.wait()
    ones = jnp.ones((16, TILE), jnp.bfloat16)

    def chunk_step(chunk, carry):
        @pl.when(chunk + AHEAD < chunks)
        def _():
            mask_copy(chunk + AHEAD).start()
            start_picks(chunk + AHEAD)

        span = pl.ds(chunk * CHUNK, CHUNK)
        mask_copy(chunk).wait()
        pltpu.make_async_copy(picked.at[span], picked.at[span], pick_sem.at[chunk]).wait()
        for k in range(CHUNK):
            tile = chunk * CHUNK + k
            values = picked[tile]
            high = values.astype(jnp.bfloat16)
            low = (values - high.astype(jnp.float32)).astype(jnp.bfloat16)
            stacked = jnp.concatenate([high, low, ones], axis=0)
            links = mask_buf[tile].astype(jnp.float32).astype(jnp.bfloat16)
            sums = lax.dot_general(
                stacked, links, (((1,), (1,)), ((), ())), preferred_element_type=jnp.float32
            )
            target = pl.ds(pl.multiple_of(rows[tile] * TILE, TILE), TILE)
            total[:, target] += sums[:feat_cols] + sums[feat_cols : 2 * feat_cols]
            degree[:, target] += sums[2 * feat_cols : 2 * feat_cols + 8]
        return carry

    lax.fori_loop(0, chunks, chunk_step, 0)

    def finish(peer, carry):
        span = pl.ds(pl.multiple_of(peer * block, block), block)
        scale = 1.0 / (degree[:, span] + 1.0)
        mean = total[:, span].reshape(feat_cols // 8, 8, block) * scale[None]
        hidden[peer] = mean.reshape(feat_cols, block).astype(jnp.bfloat16)
        return carry

    lax.fori_loop(0, peers, finish, 0)


def aggregate(features, tile_rows, tile_cols, tile_masks, peers):
    feat_cols = features.shape[0]
    tiles = tile_masks.shape[0]
    chunks = tiles // CHUNK
    return pl.pallas_call(
        aggregate_kernel,
        out_shape=jax.ShapeDtypeStruct((peers, feat_cols, NT // peers), jnp.bfloat16),
        in_specs=[
            pl.BlockSpec(memory_space=pltpu.HBM),
            pl.BlockSpec(memory_space=pltpu.HBM),
            pl.BlockSpec(memory_space=pltpu.HBM),
            pl.BlockSpec(memory_space=pltpu.HBM),
        ],
        out_specs=pl.BlockSpec(memory_space=pltpu.VMEM),
        scratch_shapes=[
            pltpu.SMEM((tiles,), jnp.int32),
            pltpu.SMEM((tiles,), jnp.int32),
            pltpu.VMEM((feat_cols, NT), jnp.float32),
            pltpu.VMEM((8, NT), jnp.float32),
            pltpu.VMEM((tiles, feat_cols, TILE), jnp.float32),
            pltpu.VMEM((tiles, TILE, TILE), jnp.int32),
            pltpu.SemaphoreType.DMA((2,)),
            pltpu.SemaphoreType.DMA,
            pltpu.SemaphoreType.DMA((chunks,)),
            pltpu.SemaphoreType.DMA((chunks,)),
        ],
        compiler_params=pltpu.CompilerParams(vmem_limit_bytes=32 << 20),
        name="aggregate",
    )(
        *(
            pltpu.with_memory_space_constraint(operand, pltpu.HBM)
            for operand in (tile_rows, tile_cols, features, tile_masks)
        )
    )


def layer_kernel(hidden, weight, upstream, activation, partial):
    peers, feat_cols, block = hidden.shape
    features = hidden[...].reshape(peers * feat_cols, block)
    preact = lax.dot_general(
        features, weight[...], (((0,), (0,)), ((), ())), preferred_element_type=jnp.float32
    )
    phi = 0.5 * (1.0 + lax.erf(preact * 0.7071067811865476))
    activation[...] = (preact * phi).astype(jnp.bfloat16)
    slope = phi + preact * jnp.exp(-0.5 * preact * preact) * 0.3989422804014327
    slopes = (upstream[...].astype(jnp.float32) * slope).astype(jnp.bfloat16)
    grad = jnp.dot(features, slopes, preferred_element_type=jnp.float32)
    partial[...] = grad.astype(jnp.bfloat16).reshape(partial.shape)


def layer(hidden, weight, upstream):
    peers, feat_cols, _ = hidden.shape
    out = weight.shape[1]
    return pl.pallas_call(
        layer_kernel,
        out_shape=(
            jax.ShapeDtypeStruct(upstream.shape, jnp.bfloat16),
            jax.ShapeDtypeStruct((peers, feat_cols, out), jnp.bfloat16),
        ),
        in_specs=[pl.BlockSpec(memory_space=pltpu.VMEM)] * 3,
        out_specs=[pl.BlockSpec(memory_space=pltpu.VMEM)] * 2,
        compiler_params=pltpu.CompilerParams(vmem_limit_bytes=32 << 20),
        name="layer",
    )(hidden, weight, upstream)


def per_device(features, tile_rows, tile_cols, tile_masks, weight, upstream):
    peers = weight.shape[0] // features.shape[0]
    hidden = aggregate(features, tile_rows, tile_cols, tile_masks, peers)
    hidden = lax.all_to_all(hidden, "feat", 0, 0)
    activation, partial = layer(hidden, weight, upstream)
    partial = lax.all_to_all(partial, "feat", 0, 0)
    local_grad = jnp.sum(partial.astype(jnp.float32), axis=0)
    weight_grad = lax.psum(local_grad, "mb")
    return (activation, weight_grad)


def solution(mesh):
    return jax.shard_map(
        per_device,
        mesh=mesh,
        in_specs=(
            P("feat", "mb"),
            P("mb"),
            P("mb"),
            P("mb", None, None),
            P(),
            P(("mb", "feat"), None),
        ),
        out_specs=(P(("mb", "feat"), None), P("feat", None)),
        check_vma=False,
    )
```

time: 274 us -> 70.6 us (0.26)
  waiting for transfers between devices: 170 us -> 0 us
  matrix products: 40.6 us -> 0 us
  blocking collectives: 17.6 us -> 58.2 us
  local copies, waits for them, and re-layouts: 15.6 us -> 0.01 us
  other arithmetic: 14.9 us -> 0.08 us
  between operations: 14.1 us -> 0.66 us
  Pallas kernels: 0 us -> 11.4 us
    reduce_scatter x1 -> x0, waiting for transfers between devices: 118 us -> none  [per_device(): lax.psum_scatter(lax.dot_general(picked, weight_part, (((0,), (0,)), ((),...]
    all_gather x1 -> x0, waiting for transfers between devices: 52.2 us -> none  [per_device(): lax.all_gather(slopes, 'feat', axis=0, tiled=True)]
    dot_general x5 -> x0, matrix products: 40.6 us -> none  [the longest x1 22.4 us: neighbor_mean(): jnp.einsum('fts,tds->tfd', picked, weights, precision=lax.Precision.HIGHEST)]
    all_to_all x0 -> x2, blocking collectives: none -> 40.3 us  [the longest x1 25.3 us: per_device(): hidden = lax.all_to_all(hidden, 'feat', 0, 0)]
    pallas_call x0 -> x2, Pallas kernels: none -> 11.4 us  [the longest x1 9.84 us: aggregate(): pl.pallas_call(aggregate_kernel, out_shape=jax.ShapeDtypeStruct((peers, f...]
    reshape x1 -> x0, local copies, waits for them, and re-layouts: 7.81 us -> none  [neighbor_mean(): blocks = sources.reshape(feat_cols, src_count // tile_size, tile_size)]
    reduce_sum x1, other arithmetic: 7.89 us -> 0.08 us  [per_device(): local_grad = jnp.sum(partial.astype(jnp.float32), axis=0)]
    gather x1 -> x0, local copies, waits for them, and re-layouts: 5.89 us -> none  [neighbor_mean(): picked = jnp.take(blocks, col_index, axis=1)]
  transfers between devices with their start and end apart: 2 -> 0, of which waited for: 2 -> 0; matrix products, arithmetic and copies ran while one was open for 0% -> 0% of each run, Pallas kernels for 0% -> 0%
where the time goes in v1:
time: 70.6 us; the launch traced here: 70.4 us
  blocking collectives  58.2 us (82%)
  Pallas kernels  11.4 us (16%)
    all_to_all x1, blocking collectives, per_device(): hidden = lax.all_to_all(hidden, 'feat', 0, 0)  25.3 us
    psum x1, blocking collectives, per_device(): weight_grad = lax.psum(local_grad, 'mb')  17.9 us
    all_to_all x1, blocking collectives, per_device(): partial = lax.all_to_all(partial, 'feat', 0, 0)  15 us
    pallas_call x1, Pallas kernels, aggregate(): pl.pallas_call(aggregate_kernel, out_shape=jax.ShapeDtypeStruct((peers, f...  9.84 us
    pallas_call x1, Pallas kernels, layer(): pl.pallas_call(layer_kernel, out_shape=(jax.ShapeDtypeStruct(upstream.sha...  1.55 us

profile of v1, /device:TPU:0, one launch (start us, length us, event | category | flops | bytes accessed | tf_op | source)
XLA Modules:
  0.0 70.4 jit_solution(878585077456202134)
XLA Ops:
  0.6 0.0 copy-start.1
  0.6 0.0 copy-start
  0.7 9.8 %aggregate.1 = bf16[32,32,512]{2,1,0:T(8,128)(2,1)S(1)} custom-call(s32[192]{0:T(256)} %row_index.1, s32[192]{0:T(256)} %col_index.1, f32[32,65536]{1,0:T(8,128)} %features.1, s32[192,128,128]{2,1,0:T(8,128)} %masks.1), custom_call_target="tpu_custom_call" | custom-call | tf_op jit(solution)/shard_map/aggregate/pallas_call | solution.py:104
  10.5 25.3 %all_to_all.10.hidden = bf16[32,32,512]{2,1,0:T(8,128)(2,1)S(1)} all-to-all(bf16[32,32,512]{2,1,0:T(8,128)(2,1)S(1)} %aggregate.1), channel_id=1, replica_groups=mesh['mb'=4,'feat'=32] {'feat'}, dimensions={0} | all-to-all | bytes 2097152 | tf_op jit(solution)/shard_map/all_to_all | solution.py:169
  35.8 0.0 copy-done.1
  35.8 0.0 copy-done
  35.8 1.6 %layer.1 = (bf16[512,256]{1,0:T(8,128)(2,1)}, bf16[32,32,256]{2,1,0:T(8,128)(2,1)S(1)}) custom-call(bf16[32,32,512]{2,1,0:T(8,128)(2,1)S(1)} %all_to_all.10.hidden, bf16[1024,256]{1,0:T(8,128)(2,1)S(1)} %copy-done, bf16[512,256]{1,0:T(8,128)(2,1)S(1)} %copy-done.1), custom_call_target="tpu_custom_call" | custom-call | tf_op jit(solution)/shard_map/layer/pallas_call | solution.py:153
  37.3 15.0 %all_to_all.11 = bf16[32,32,256]{2,1,0:T(8,128)(2,1)S(1)} all-to-all(bf16[32,32,256]{2,1,0:T(8,128)(2,1)S(1)} %get-tuple-element.5), channel_id=1, replica_groups=mesh['mb'=4,'feat'=32] {'feat'}, dimensions={0} | all-to-all | bytes 1048576 | tf_op jit(solution)/shard_map/all_to_all | solution.py:171
  52.4 0.1 convert_reduce_fusion
  52.5 17.9 %psum.7 = f32[32,256]{1,0:T(8,128)} all-reduce(f32[32,256]{1,0:T(8,128)S(1)} %convert_reduce_fusion), channel_id=1, replica_groups=mesh['mb'=4,'feat'=32] {'mb'}, use_global_device_ids=true, to_apply=%region_1.0 | all-reduce | flops 8192 | bytes 65536 | tf_op jit(solution)/shard_map/psum | solution.py:173
Async XLA Ops:
  0.6 35.2 %copy-start.1 = (bf16[512,256]{1,0:T(8,128)(2,1)S(1)}, bf16[512,256]{1,0:T(8,128)(2,1)}, u32[]{:S(2)}) copy-start(bf16[512,256]{1,0:T(8,128)(2,1)} %upstream.1) | copy-start | bytes 786436
  0.6 35.1 %copy-start = (bf16[1024,256]{1,0:T(8,128)(2,1)S(1)}, bf16[1024,256]{1,0:T(8,128)(2,1)}, u32[]{:S(2)}) copy-start(bf16[1024,256]{1,0:T(8,128)(2,1)} %weight.1) | copy-start | bytes 1572868

commit v2 on v1

v2 whole, which is shorter than its diff:
```python
import jax
import jax.numpy as jnp
from jax import lax
from jax.experimental import pallas as pl
from jax.experimental.pallas import tpu as pltpu
from jax.sharding import Mesh
from jax.sharding import PartitionSpec as P

NT = 16384
N_MB = 4
CORES = 2
FEAT = ("z", "x", "core")
TILE = 128
CHUNK = 32
AHEAD = 3
FINISH = 8


def aggregate_kernel(
    row_index,
    col_index,
    features,
    masks,
    hidden,
    rows,
    cols,
    own,
    total,
    degree,
    picked,
    mask_buf,
    index_sem,
    self_sem,
    pick_sem,
    mask_sem,
):
    feat_cols = features.shape[0]
    chunks = mask_buf.shape[0] // CHUNK
    peers, _, block = hidden.shape

    def mask_copy(chunk):
        span = pl.ds(chunk * CHUNK, CHUNK)
        return pltpu.make_async_copy(masks.at[span], mask_buf.at[span], mask_sem.at[chunk])

    def start_pick(chunk, k):
        tile = chunk * CHUNK + k
        first = pl.multiple_of(cols[tile] * TILE, TILE)
        pltpu.make_async_copy(
            features.at[:, pl.ds(first, TILE)], picked.at[tile], pick_sem.at[chunk]
        ).start()

    fetch_rows = pltpu.make_async_copy(row_index, rows, index_sem.at[0])
    fetch_cols = pltpu.make_async_copy(col_index, cols, index_sem.at[1])
    fetch_own = pltpu.make_async_copy(features.at[:, pl.ds(0, NT)], own, self_sem)
    fetch_cols.start()
    fetch_rows.start()
    mask_copy(0).start()
    total[...] = jnp.zeros_like(total)
    degree[...] = jnp.zeros_like(degree)
    fetch_cols.wait()
    fetch_rows.wait()
    for chunk in range(AHEAD):
        if chunk:
            mask_copy(chunk).start()
        for k in range(CHUNK):
            start_pick(chunk, k)
    fetch_own.start()
    counter = jnp.concatenate(
        [jnp.ones((16, TILE), jnp.bfloat16), jnp.zeros((16, TILE), jnp.bfloat16)], axis=1
    )

    def chunk_step(chunk, prefetch):
        span = pl.ds(chunk * CHUNK, CHUNK)
        if prefetch:
            mask_copy(chunk + AHEAD).start()
        mask_copy(chunk).wait()
        pltpu.make_async_copy(picked.at[span], picked.at[span], pick_sem.at[chunk]).wait()
        for k in range(CHUNK):
            if prefetch:
                start_pick(chunk + AHEAD, k)
            tile = chunk * CHUNK + k
            values = picked[tile]
            high = values.astype(jnp.bfloat16)
            low = (values - high.astype(jnp.float32)).astype(jnp.bfloat16)
            halves = jnp.concatenate([jnp.concatenate([high, low], axis=1), counter], axis=0)
            links = mask_buf[tile].astype(jnp.float32).astype(jnp.bfloat16).T
            sums = jnp.dot(
                halves,
                jnp.concatenate([links, links], axis=0),
                preferred_element_type=jnp.float32,
            )
            target = pl.ds(pl.multiple_of(rows[tile] * TILE, TILE), TILE)
            total[:, target] += sums[:feat_cols]
            degree[:, target] += sums[feat_cols : feat_cols + 8]

    @pl.loop(0, chunks - AHEAD)
    def _(chunk):
        chunk_step(chunk, True)

    @pl.loop(chunks - AHEAD, chunks)
    def _(chunk):
        chunk_step(chunk, False)

    fetch_own.wait()

    @pl.loop(0, peers // FINISH)
    def _(step):
        for k in range(FINISH):
            peer = step * FINISH + k
            span = pl.ds(pl.multiple_of(peer * block, block), block)
            scale = 1.0 / (degree[:, span] + 1.0)
            mean = (total[:, span] + own[:, span]).reshape(feat_cols // 8, 8, block) * scale[None]
            hidden[peer] = mean.reshape(feat_cols, block).astype(jnp.bfloat16)


def aggregate(features, tile_rows, tile_cols, tile_masks, peers):
    feat_cols = features.shape[0]
    tiles = tile_masks.shape[0]
    chunks = tiles // CHUNK
    return pl.pallas_call(
        aggregate_kernel,
        out_shape=jax.ShapeDtypeStruct((peers, feat_cols, NT // peers), jnp.bfloat16),
        in_specs=[
            pl.BlockSpec(memory_space=pltpu.HBM),
            pl.BlockSpec(memory_space=pltpu.HBM),
            pl.BlockSpec(memory_space=pltpu.HBM),
            pl.BlockSpec(memory_space=pltpu.HBM),
        ],
        out_specs=pl.BlockSpec(memory_space=pltpu.VMEM),
        scratch_shapes=[
            pltpu.SMEM((tiles,), jnp.int32),
            pltpu.SMEM((tiles,), jnp.int32),
            pltpu.VMEM((feat_cols, NT), jnp.float32),
            pltpu.VMEM((feat_cols, NT), jnp.float32),
            pltpu.VMEM((8, NT), jnp.float32),
            pltpu.VMEM((tiles, feat_cols, TILE), jnp.float32),
            pltpu.VMEM((tiles, TILE, TILE), jnp.int32),
            pltpu.SemaphoreType.DMA((2,)),
            pltpu.SemaphoreType.DMA,
            pltpu.SemaphoreType.DMA((chunks,)),
            pltpu.SemaphoreType.DMA((chunks,)),
        ],
        compiler_params=pltpu.CompilerParams(vmem_limit_bytes=32 << 20),
        name="aggregate",
    )(
        *(
            pltpu.with_memory_space_constraint(operand, pltpu.HBM)
            for operand in (tile_rows, tile_cols, features, tile_masks)
        )
    )


def layer_kernel(hidden, weight, upstream, activation, kept, sent):
    chips, cores, feat_cols, block = hidden.shape
    features = hidden[...].reshape(chips * cores * feat_cols, block)
    preact = lax.dot_general(
        features, weight[...], (((0,), (0,)), ((), ())), preferred_element_type=jnp.float32
    )
    phi = 0.5 * (1.0 + lax.erf(preact * 0.7071067811865476))
    activation[...] = (preact * phi).astype(jnp.bfloat16)
    slope = phi + preact * jnp.exp(-0.5 * preact * preact) * 0.3989422804014327
    slopes = (upstream[...].astype(jnp.float32) * slope).astype(jnp.bfloat16)
    core = lax.axis_index("core")
    for part, owner in ((sent, 1 - core), (kept, core)):
        rows = hidden[:, owner].reshape(chips * feat_cols, block)
        grad = jnp.dot(rows, slopes, preferred_element_type=jnp.float32)
        part[...] = grad.astype(part.dtype).reshape(part.shape)


def layer(hidden, weight, upstream):
    chips, cores, feat_cols, _ = hidden.shape
    out = weight.shape[1]
    return pl.pallas_call(
        layer_kernel,
        out_shape=(
            jax.ShapeDtypeStruct(upstream.shape, jnp.bfloat16),
            jax.ShapeDtypeStruct((chips, feat_cols, out), jnp.float32),
            jax.ShapeDtypeStruct((chips, feat_cols, out), jnp.bfloat16),
        ),
        in_specs=[pl.BlockSpec(memory_space=pltpu.VMEM)] * 3,
        out_specs=[pl.BlockSpec(memory_space=pltpu.VMEM)] * 3,
        compiler_params=pltpu.CompilerParams(vmem_limit_bytes=32 << 20),
        name="layer",
    )(hidden, weight, upstream)


def per_device(features, tile_rows, tile_cols, tile_masks, weight, upstream):
    peers = weight.shape[0] // features.shape[0]
    hidden = aggregate(features, tile_rows, tile_cols, tile_masks, peers)
    hidden = lax.all_to_all(hidden, FEAT, 0, 0)
    hidden = hidden.reshape(peers // CORES, CORES, *hidden.shape[1:])
    activation, kept, sent = layer(hidden, weight, upstream)
    partial = (kept + lax.ppermute(sent, "core", [(0, 1), (1, 0)])).astype(jnp.bfloat16)
    partial = lax.all_to_all(partial, ("z", "x"), 0, 0)
    local_grad = jnp.sum(partial.astype(jnp.float32), axis=0)
    weight_grad = local_grad
    for shift in range(1, N_MB):
        ring = [(member, (member + shift) % N_MB) for member in range(N_MB)]
        weight_grad += lax.ppermute(local_grad, "mb", ring)
    return (activation, weight_grad)


def solution(mesh):
    side = mesh.shape["feat"] // CORES
    side = int(side**0.5)
    mesh = Mesh(
        mesh.devices.reshape(mesh.shape["mb"], side, side, CORES), ("mb",) + FEAT
    )
    return jax.shard_map(
        per_device,
        mesh=mesh,
        in_specs=(
            P(FEAT, "mb"),
            P("mb"),
            P("mb"),
            P("mb", None, None),
            P(),
            P(("mb",) + FEAT, None),
        ),
        out_specs=(P(("mb",) + FEAT, None), P(FEAT, None)),
        check_vma=False,
    )
```

time: 70.6 us -> 59.1 us (0.84)
  blocking collectives: 58.2 us -> 37.7 us
  waiting for transfers between devices: 0 us -> 5.6 us
  starting transfers between devices: 0 us -> 4.79 us
  Pallas kernels: 11.4 us -> 9.39 us
    psum x1 -> x0, blocking collectives: 17.9 us -> none  [per_device(): weight_grad = lax.psum(local_grad, 'mb')]
    ppermute x0 -> x4, waiting for transfers between devices: none -> 5.6 us  [the longest x3 4.18 us: per_device(): weight_grad += lax.ppermute(local_grad, 'mb', ring)]
    ppermute x0 -> x4, starting transfers between devices: none -> 4.79 us  [the longest x3 4.67 us: per_device(): weight_grad += lax.ppermute(local_grad, 'mb', ring)]
    all_to_all x2, blocking collectives: 40.3 us -> 37.7 us  [the longest x1 25.3 us: per_device(): hidden = lax.all_to_all(hidden, FEAT, 0, 0)]
    pallas_call x1, Pallas kernels: 9.84 us -> 7.52 us  [aggregate(): pl.pallas_call(aggregate_kernel, out_shape=jax.ShapeDtypeStruct((peers, f...]
  transfers between devices with their start and end apart: 0 -> 4, of which waited for: 0 -> 3; matrix products, arithmetic and copies ran while one was open for 0% -> 0% of each run, Pallas kernels for 0% -> 0%
where the time goes in v2:
time: 59.1 us; the launch traced here: 58.9 us
  blocking collectives  37.7 us (64%)
  Pallas kernels  9.39 us (16%)
  waiting for transfers between devices  5.6 us (9%)
  starting transfers between devices  4.79 us (8%)
  other arithmetic  0.74 us (1%)
  between operations  0.67 us (1%)
    all_to_all x1, blocking collectives, per_device(): hidden = lax.all_to_all(hidden, FEAT, 0, 0)  25.3 us
    all_to_all x1, blocking collectives, per_device(): partial = lax.all_to_all(partial, ('z', 'x'), 0, 0)  12.4 us
    pallas_call x1, Pallas kernels, aggregate(): pl.pallas_call(aggregate_kernel, out_shape=jax.ShapeDtypeStruct((peers, f...  7.52 us
    ppermute x3, starting transfers between devices, per_device(): weight_grad += lax.ppermute(local_grad, 'mb', ring)  4.67 us
    ppermute x3, waiting for transfers between devices, per_device(): weight_grad += lax.ppermute(local_grad, 'mb', ring)  4.18 us
    pallas_call x1, Pallas kernels, layer(): pl.pallas_call(layer_kernel, out_shape=(jax.ShapeDtypeStruct(upstream.sha...  1.88 us
    ppermute x1, waiting for transfers between devices, per_device(): lax.ppermute(sent, 'core', [(0, 1), (1, 0)])  1.42 us
  transfers between devices with their start and end apart: 4, of which 3 were waited for; matrix products, arithmetic and copies ran while one was open for 0% of the time, Pallas kernels for 0%

profile of v2, /device:TPU:0, one launch (start us, length us, event | category | flops | bytes accessed | tf_op | source)
XLA Modules:
  0.0 58.9 jit_solution(6877663517956328877)
XLA Ops:
  0.6 0.0 copy-start.1
  0.6 0.0 copy-start
  0.7 7.5 %aggregate.1 = bf16[32,32,512]{2,1,0:T(8,128)(2,1)S(1)} custom-call(s32[192]{0:T(256)} %row_index.1, s32[192]{0:T(256)} %col_index.1, f32[32,65536]{1,0:T(8,128)} %features.1, s32[192,128,128]{2,1,0:T(8,128)} %masks.1), custom_call_target="tpu_custom_call" | custom-call | tf_op jit(solution)/shard_map/aggregate/pallas_call | solution.py:120
  8.2 25.3 %all_to_all.10 = bf16[32,32,512]{2,1,0:T(8,128)(2,1)S(1)} all-to-all(bf16[32,32,512]{2,1,0:T(8,128)(2,1)S(1)} %aggregate.1), channel_id=1, replica_groups=mesh['mb'=4,'z'=4,'x'=4,'core'=2] {'z','x','core'}, dimensions={0} | all-to-all | bytes 2097152 | tf_op jit(solution)/shard_map/all_to_all | solution.py:190
  33.5 0.0 copy-done.1
  33.5 0.0 copy-done
  33.5 1.9 %layer.1 = (bf16[512,256]{1,0:T(8,128)(2,1)}, f32[16,32,256]{2,1,0:T(8,128)S(1)}, bf16[16,32,256]{2,1,0:T(8,128)(2,1)S(1)}) custom-call(bf16[16,2,32,512]{3,2,1,0:T(8,128)(2,1)S(1)} %bitcast.1, bf16[1024,256]{1,0:T(8,128)(2,1)S(1)} %copy-done, bf16[512,256]{1,0:T(8,128)(2,1)S(1)} %copy-done.1), custom_call_target="tpu_custom_call" | custom-call | tf_op jit(solution)/shard_map/layer/pallas_call | solution.py:173
  35.3 0.1 collective-permute-start
  35.5 1.4 %collective-permute-done = bf16[16,32,256]{2,1,0:T(8,128)(2,1)S(1)} collective-permute-done((bf16[16,32,256]{2,1,0:T(8,128)(2,1)S(1)}, bf16[16,32,256]{2,1,0:T(8,128)(2,1)S(1)}, u32[]{:S(2)}, u32[]{:S(2)}) %collective-permute-start) | collective-permute-done | bytes 262176 | tf_op jit(solution)/shard_map/ppermute | solution.py:193
  36.9 0.1 add_convert_fusion
  37.0 12.4 %all_to_all.11 = bf16[16,32,256]{2,1,0:T(8,128)(2,1)S(1)} all-to-all(bf16[16,32,256]{2,1,0:T(8,128)(2,1)S(1)} %add_convert_fusion), channel_id=1, replica_groups=mesh['mb'=4,'z'=4,'x'=4,'core'=2] {'z','x'}, dimensions={0} | all-to-all | bytes 524288 | tf_op jit(solution)/shard_map/all_to_all | solution.py:194
  49.4 3.1 %collective-permute-start.3 = (f32[32,256]{1,0:T(8,128)S(1)}, f32[32,256]{1,0:T(8,128)S(1)}, u32[]{:S(2)}, u32[]{:S(2)}) collective-permute-start(f32[32,256]{1,0:T(8,128)S(1)} %convert_reduce_fusion), channel_id=1, source_target_pairs={{0,96},{32,0},{64,32},{96,64},{1,97},{33,1},{65,33},{97,65},{2,98}... | collective-permute-start | bytes 98312 | tf_op jit(solution)/shard_map/ppermute | solution.py:199
  52.5 0.6 %collective-permute-start.2 = (f32[32,256]{1,0:T(8,128)S(1)}, f32[32,256]{1,0:T(8,128)S(1)}, u32[]{:S(2)}, u32[]{:S(2)}) collective-permute-start(f32[32,256]{1,0:T(8,128)S(1)} %convert_reduce_fusion), channel_id=1, source_target_pairs={{0,64},{32,96},{64,0},{96,32},{1,65},{33,97},{65,1},{97,33},{2,66}... | collective-permute-start | bytes 98312 | tf_op jit(solution)/shard_map/ppermute | solution.py:199
  53.1 1.0 %collective-permute-start.1 = (f32[32,256]{1,0:T(8,128)S(1)}, f32[32,256]{1,0:T(8,128)S(1)}, u32[]{:S(2)}, u32[]{:S(2)}) collective-permute-start(f32[32,256]{1,0:T(8,128)S(1)} %convert_reduce_fusion), channel_id=1, source_target_pairs={{0,32},{32,64},{64,96},{96,0},{1,33},{33,65},{65,97},{97,1},{2,34}... | collective-permute-start | bytes 98312 | tf_op jit(solution)/shard_map/ppermute | solution.py:199
  54.1 0.0 collective-permute-done.3
  54.1 3.8 %collective-permute-done.2 = f32[32,256]{1,0:T(8,128)S(1)} collective-permute-done((f32[32,256]{1,0:T(8,128)S(1)}, f32[32,256]{1,0:T(8,128)S(1)}, u32[]{:S(2)}, u32[]{:S(2)}) %collective-permute-start.2) | collective-permute-done | bytes 32800 | tf_op jit(solution)/shard_map/ppermute | solution.py:199
  57.9 0.4 collective-permute-done.1
  58.3 0.6 %add_add_fusion = f32[32,256]{1,0:T(8,128)} fusion(f32[32,256]{1,0:T(8,128)S(1)} %collective-permute-done.3, f32[32,256]{1,0:T(8,128)S(1)} %collective-permute-done.2, f32[32,256]{1,0:T(8,128)S(1)} %convert_reduce_fusion, f32[32,256]{1,0:T(8,128)S(1)} %collective-permute-done.1), kind=kLoop, calls=%fused_computation.2 | loop fusion | flops 24576 | bytes 163840 | tf_op jit(solution)/shard_map/add | solution.py:199
  (1 shorter events, 0.0 us)
Async XLA Ops:
  0.6 32.8 %copy-start.1 = (bf16[512,256]{1,0:T(8,128)(2,1)S(1)}, bf16[512,256]{1,0:T(8,128)(2,1)}, u32[]{:S(2)}) copy-start(bf16[512,256]{1,0:T(8,128)(2,1)} %upstream.1) | copy-start | bytes 786436
  0.6 32.8 %copy-start = (bf16[1024,256]{1,0:T(8,128)(2,1)S(1)}, bf16[1024,256]{1,0:T(8,128)(2,1)}, u32[]{:S(2)}) copy-start(bf16[1024,256]{1,0:T(8,128)(2,1)} %weight.1) | copy-start | bytes 1572868
  35.3 1.5 %collective-permute-start = (bf16[16,32,256]{2,1,0:T(8,128)(2,1)S(1)}, bf16[16,32,256]{2,1,0:T(8,128)(2,1)S(1)}, u32[]{:S(2)}, u32[]{:S(2)}) collective-permute-start(bf16[16,32,256]{2,1,0:T(8,128)(2,1)S(1)} %get-tuple-element.7), channel_id=1, source_target_pairs={{0,1},{1,0},{2,3},{3,2},{4,5},{5,4},{6,7},{7,6},{8,9},{9,8},{10,11... | collective-permute-start | bytes 786440 | tf_op jit(solution)/shard_map/ppermute | solution.py:193
  49.4 4.7 %collective-permute-start.3 = (f32[32,256]{1,0:T(8,128)S(1)}, f32[32,256]{1,0:T(8,128)S(1)}, u32[]{:S(2)}, u32[]{:S(2)}) collective-permute-start(f32[32,256]{1,0:T(8,128)S(1)} %convert_reduce_fusion), channel_id=1, source_target_pairs={{0,96},{32,0},{64,32},{96,64},{1,97},{33,1},{65,33},{97,65},{2,98}... | collective-permute-start | bytes 98312 | tf_op jit(solution)/shard_map/ppermute | solution.py:199
  52.5 5.4 %collective-permute-start.2 = (f32[32,256]{1,0:T(8,128)S(1)}, f32[32,256]{1,0:T(8,128)S(1)}, u32[]{:S(2)}, u32[]{:S(2)}) collective-permute-start(f32[32,256]{1,0:T(8,128)S(1)} %convert_reduce_fusion), channel_id=1, source_target_pairs={{0,64},{32,96},{64,0},{96,32},{1,65},{33,97},{65,1},{97,33},{2,66}... | collective-permute-start | bytes 98312 | tf_op jit(solution)/shard_map/ppermute | solution.py:199
  53.1 5.1 %collective-permute-start.1 = (f32[32,256]{1,0:T(8,128)S(1)}, f32[32,256]{1,0:T(8,128)S(1)}, u32[]{:S(2)}, u32[]{:S(2)}) collective-permute-start(f32[32,256]{1,0:T(8,128)S(1)} %convert_reduce_fusion), channel_id=1, source_target_pairs={{0,32},{32,64},{64,96},{96,0},{1,33},{33,65},{65,97},{97,1},{2,34}... | collective-permute-start | bytes 98312 | tf_op jit(solution)/shard_map/ppermute | solution.py:199

commit v3 on v2

--- a/solution.py
+++ b/solution.py
@@ -13,7 +13,7 @@
 TILE = 128
 CHUNK = 32
 AHEAD = 3
-FINISH = 8
+FINISH = 16
 
 
 def aggregate_kernel(
@@ -55,16 +55,16 @@
     fetch_cols.start()
     fetch_rows.start()
     mask_copy(0).start()
+    mask_copy(1).start()
     total[...] = jnp.zeros_like(total)
     degree[...] = jnp.zeros_like(degree)
     fetch_cols.wait()
     fetch_rows.wait()
     for chunk in range(AHEAD):
-        if chunk:
+        if chunk > 1:
             mask_copy(chunk).start()
         for k in range(CHUNK):
             start_pick(chunk, k)
-    fetch_own.start()
     counter = jnp.concatenate(
         [jnp.ones((16, TILE), jnp.bfloat16), jnp.zeros((16, TILE), jnp.bfloat16)], axis=1
     )
@@ -97,6 +97,8 @@
     def _(chunk):
         chunk_step(chunk, True)
 
+    fetch_own.start()
+
     @pl.loop(chunks - AHEAD, chunks)
     def _(chunk):
         chunk_step(chunk, False)
@@ -150,38 +152,72 @@
     )
 
 
-def layer_kernel(hidden, weight, upstream, activation, kept, sent):
+def gate(preact):
+    return 0.5 * (1.0 + lax.erf(preact * 0.7071067811865476))
+
+
+def slopes_kernel(hidden, weight, upstream, preact, slopes, sent):
     chips, cores, feat_cols, block = hidden.shape
-    features = hidden[...].reshape(chips * cores * feat_cols, block)
-    preact = lax.dot_general(
-        features, weight[...], (((0,), (0,)), ((), ())), preferred_element_type=jnp.float32
-    )
-    phi = 0.5 * (1.0 + lax.erf(preact * 0.7071067811865476))
-    activation[...] = (preact * phi).astype(jnp.bfloat16)
-    slope = phi + preact * jnp.exp(-0.5 * preact * preact) * 0.3989422804014327
-    slopes = (upstream[...].astype(jnp.float32) * slope).astype(jnp.bfloat16)
-    core = lax.axis_index("core")
-    for part, owner in ((sent, 1 - core), (kept, core)):
-        rows = hidden[:, owner].reshape(chips * feat_cols, block)
-        grad = jnp.dot(rows, slopes, preferred_element_type=jnp.float32)
-        part[...] = grad.astype(part.dtype).reshape(part.shape)
+    for first in range(0, block, TILE):
+        span = slice(first, first + TILE)
+        features = hidden[:, :, :, span].reshape(chips * cores * feat_cols, TILE)
+        value = jnp.dot(features.T, weight[...], preferred_element_type=jnp.float32)
+        preact[span] = value
+        slope = gate(value) + value * jnp.exp(-0.5 * value * value) * 0.3989422804014327
+        slopes[span] = (upstream[span].astype(jnp.float32) * slope).astype(jnp.bfloat16)
+    rows = hidden[:, 1 - lax.axis_index("core")].reshape(chips * feat_cols, block)
+    grad = jnp.dot(rows, slopes[...], preferred_element_type=jnp.float32)
+    sent[...] = grad.astype(jnp.bfloat16).reshape(sent.shape)
+
+
+def rest_kernel(hidden, preact, slopes, activation, kept):
+    chips, cores, feat_cols, block = hidden.shape
+    rows = hidden[:, lax.axis_index("core")].reshape(chips * feat_cols, block)
+    grad = jnp.dot(rows, slopes[...], preferred_element_type=jnp.float32)
+    kept[...] = grad.reshape(kept.shape)
+    activation[...] = (preact[...] * gate(preact[...])).astype(jnp.bfloat16)
+
+
+def call_in_vmem(kernel, name, outputs, *operands):
+    in_vmem = pl.BlockSpec(memory_space=pltpu.VMEM)
+    return pl.pallas_call(
+        kernel,
+        out_shape=outputs,
+        in_specs=[in_vmem] * len(operands),
+        out_specs=[in_vmem] * len(outputs),
+        compiler_params=pltpu.CompilerParams(vmem_limit_bytes=32 << 20),
+        name=name,
+    )(*operands)
 
 
 def layer(hidden, weight, upstream):
     chips, cores, feat_cols, _ = hidden.shape
-    out = weight.shape[1]
-    return pl.pallas_call(
-        layer_kernel,
-        out_shape=(
+    grad_shape = (chips, feat_cols, weight.shape[1])
+    preact, slopes, sent = call_in_vmem(
+        slopes_kernel,
+        "slopes",
+        (
+            jax.ShapeDtypeStruct(upstream.shape, jnp.float32),
             jax.ShapeDtypeStruct(upstream.shape, jnp.bfloat16),
-            jax.ShapeDtypeStruct((chips, feat_cols, out), jnp.float32),
-            jax.ShapeDtypeStruct((chips, feat_cols, out), jnp.bfloat16),
+            jax.ShapeDtypeStruct(grad_shape, jnp.bfloat16),
         ),
-        in_specs=[pl.BlockSpec(memory_space=pltpu.VMEM)] * 3,
-        out_specs=[pl.BlockSpec(memory_space=pltpu.VMEM)] * 3,
-        compiler_params=pltpu.CompilerParams(vmem_limit_bytes=32 << 20),
-        name="layer",
-    )(hidden, weight, upstream)
+        hidden,
+        weight,
+        upstream,
+    )
+    received = lax.ppermute(sent, "core", [(0, 1), (1, 0)])
+    activation, kept = call_in_vmem(
+        rest_kernel,
+        "rest",
+        (
+            jax.ShapeDtypeStruct(upstream.shape, jnp.bfloat16),
+            jax.ShapeDtypeStruct(grad_shape, jnp.float32),
+        ),
+        hidden,
+        preact,
+        slopes,
+    )
+    return activation, (kept + received).astype(jnp.bfloat16)
 
 
 def per_device(features, tile_rows, tile_cols, tile_masks, weight, upstream):
@@ -189,8 +225,7 @@
     hidden = aggregate(features, tile_rows, tile_cols, tile_masks, peers)
     hidden = lax.all_to_all(hidden, FEAT, 0, 0)
     hidden = hidden.reshape(peers // CORES, CORES, *hidden.shape[1:])
-    activation, kept, sent = layer(hidden, weight, upstream)
-    partial = (kept + lax.ppermute(sent, "core", [(0, 1), (1, 0)])).astype(jnp.bfloat16)
+    activation, partial = layer(hidden, weight, upstream)
     partial = lax.all_to_all(partial, ("z", "x"), 0, 0)
     local_grad = jnp.sum(partial.astype(jnp.float32), axis=0)
     weight_grad = local_grad

time: 59.1 us -> 57.7 us (0.976)
  waiting for transfers between devices: 5.6 us -> 4.48 us
    ppermute x1, waiting for transfers between devices: 1.42 us -> 0.32 us  [layer(): received = lax.ppermute(sent, 'core', [(0, 1), (1, 0)])]
    pallas_call x1 -> x2, Pallas kernels: 1.88 us -> 1.92 us  [call_in_vmem(): pl.pallas_call(kernel, out_shape=outputs, in_specs=[in_vmem] * len(operan...]
  transfers between devices with their start and end apart: 4 -> 4, of which waited for: 3 -> 3; matrix products, arithmetic and copies ran while one was open for 0% -> 0% of each run, Pallas kernels for 0% -> 2%
where the time goes in v3:
time: 57.7 us; the launch traced here: 57.6 us
  blocking collectives  37.7 us (65%)
  Pallas kernels  9.08 us (16%)
  starting transfers between devices  4.88 us (8%)
  waiting for transfers between devices  4.48 us (8%)
  other arithmetic  0.74 us (1%)
  between operations  0.67 us (1%)
    all_to_all x1, blocking collectives, per_device(): hidden = lax.all_to_all(hidden, FEAT, 0, 0)  25.3 us
    all_to_all x1, blocking collectives, per_device(): partial = lax.all_to_all(partial, ('z', 'x'), 0, 0)  12.4 us
    pallas_call x1, Pallas kernels, aggregate(): pl.pallas_call(aggregate_kernel, out_shape=jax.ShapeDtypeStruct((peers, f...  7.16 us
    ppermute x3, starting transfers between devices, per_device(): weight_grad += lax.ppermute(local_grad, 'mb', ring)  4.69 us
    ppermute x3, waiting for transfers between devices, per_device(): weight_grad += lax.ppermute(local_grad, 'mb', ring)  4.17 us
    pallas_call x2, Pallas kernels, call_in_vmem(): pl.pallas_call(kernel, out_shape=outputs, in_specs=[in_vmem] * len(operan...  1.92 us
  transfers between devices with their start and end apart: 4, of which 3 were waited for; matrix products, arithmetic and copies ran while one was open for 0% of the time, Pallas kernels for 2%

profile of v3, /device:TPU:0, one launch (start us, length us, event | category | flops | bytes accessed | tf_op | source)
XLA Modules:
  0.0 57.6 jit_solution(14682993855341155119)
XLA Ops:
  0.6 0.0 copy-start.1
  0.6 0.0 copy-start
  0.7 7.2 %aggregate.1 = bf16[32,32,512]{2,1,0:T(8,128)(2,1)S(1)} custom-call(s32[192]{0:T(256)} %row_index.1, s32[192]{0:T(256)} %col_index.1, f32[32,65536]{1,0:T(8,128)} %features.1, s32[192,128,128]{2,1,0:T(8,128)} %masks.1), custom_call_target="tpu_custom_call" | custom-call | tf_op jit(solution)/shard_map/aggregate/pallas_call | solution.py:122
  7.8 25.3 %all_to_all.10 = bf16[32,32,512]{2,1,0:T(8,128)(2,1)S(1)} all-to-all(bf16[32,32,512]{2,1,0:T(8,128)(2,1)S(1)} %aggregate.1), channel_id=1, replica_groups=mesh['mb'=4,'z'=4,'x'=4,'core'=2] {'z','x','core'}, dimensions={0} | all-to-all | bytes 2097152 | tf_op jit(solution)/shard_map/all_to_all | solution.py:226
  33.1 0.0 copy-done.1
  33.1 0.0 copy-done
  33.1 0.8 %slopes.1 = (f32[512,256]{1,0:T(8,128)S(1)}, bf16[512,256]{1,0:T(8,128)(2,1)S(1)}, bf16[16,32,256]{2,1,0:T(8,128)(2,1)S(1)}) custom-call(bf16[16,2,32,512]{3,2,1,0:T(8,128)(2,1)S(1)} %bitcast.1, bf16[1024,256]{1,0:T(8,128)(2,1)S(1)} %copy-done, bf16[512,256]{1,0:T(8,128)(2,1)S(1)} %copy-done.1), custom_call_target="tpu_custom_call" | custom-call | tf_op jit(solution)/shard_map/slopes/pallas_call | solution.py:183
  33.9 0.2 collective-permute-start
  34.1 1.1 %rest.1 = (bf16[512,256]{1,0:T(8,128)(2,1)}, f32[16,32,256]{2,1,0:T(8,128)S(1)}) custom-call(bf16[16,2,32,512]{3,2,1,0:T(8,128)(2,1)S(1)} %bitcast.2, f32[512,256]{1,0:T(8,128)S(1)} %get-tuple-element.7.preact, bf16[512,256]{1,0:T(8,128)(2,1)S(1)} %get-tuple-element.8.slopes), custom_call_target="tpu_custom_call" | custom-call | tf_op jit(solution)/shard_map/rest/pallas_call | solution.py:183
  35.2 0.3 collective-permute-done
  35.5 0.1 add_convert_fusion
  35.6 12.4 %all_to_all.11 = bf16[16,32,256]{2,1,0:T(8,128)(2,1)S(1)} all-to-all(bf16[16,32,256]{2,1,0:T(8,128)(2,1)S(1)} %add_convert_fusion), channel_id=1, replica_groups=mesh['mb'=4,'z'=4,'x'=4,'core'=2] {'z','x'}, dimensions={0} | all-to-all | bytes 524288 | tf_op jit(solution)/shard_map/all_to_all | solution.py:229
  48.1 3.1 %collective-permute-start.3 = (f32[32,256]{1,0:T(8,128)S(1)}, f32[32,256]{1,0:T(8,128)S(1)}, u32[]{:S(2)}, u32[]{:S(2)}) collective-permute-start(f32[32,256]{1,0:T(8,128)S(1)} %convert_reduce_fusion), channel_id=1, source_target_pairs={{0,96},{32,0},{64,32},{96,64},{1,97},{33,1},{65,33},{97,65},{2,98}... | collective-permute-start | bytes 98312 | tf_op jit(solution)/shard_map/ppermute | solution.py:234
  51.2 0.6 %collective-permute-start.2 = (f32[32,256]{1,0:T(8,128)S(1)}, f32[32,256]{1,0:T(8,128)S(1)}, u32[]{:S(2)}, u32[]{:S(2)}) collective-permute-start(f32[32,256]{1,0:T(8,128)S(1)} %convert_reduce_fusion), channel_id=1, source_target_pairs={{0,64},{32,96},{64,0},{96,32},{1,65},{33,97},{65,1},{97,33},{2,66}... | collective-permute-start | bytes 98312 | tf_op jit(solution)/shard_map/ppermute | solution.py:234
  51.8 1.0 %collective-permute-start.1 = (f32[32,256]{1,0:T(8,128)S(1)}, f32[32,256]{1,0:T(8,128)S(1)}, u32[]{:S(2)}, u32[]{:S(2)}) collective-permute-start(f32[32,256]{1,0:T(8,128)S(1)} %convert_reduce_fusion), channel_id=1, source_target_pairs={{0,32},{32,64},{64,96},{96,0},{1,33},{33,65},{65,97},{97,1},{2,34}... | collective-permute-start | bytes 98312 | tf_op jit(solution)/shard_map/ppermute | solution.py:234
  52.8 0.0 collective-permute-done.3
  52.8 3.8 %collective-permute-done.2 = f32[32,256]{1,0:T(8,128)S(1)} collective-permute-done((f32[32,256]{1,0:T(8,128)S(1)}, f32[32,256]{1,0:T(8,128)S(1)}, u32[]{:S(2)}, u32[]{:S(2)}) %collective-permute-start.2) | collective-permute-done | bytes 32800 | tf_op jit(solution)/shard_map/ppermute | solution.py:234
  56.6 0.4 collective-permute-done.1
  56.9 0.6 %add_add_fusion = f32[32,256]{1,0:T(8,128)} fusion(f32[32,256]{1,0:T(8,128)S(1)} %collective-permute-done.3, f32[32,256]{1,0:T(8,128)S(1)} %collective-permute-done.2, f32[32,256]{1,0:T(8,128)S(1)} %convert_reduce_fusion, f32[32,256]{1,0:T(8,128)S(1)} %collective-permute-done.1), kind=kLoop, calls=%fused_computation.2 | loop fusion | flops 24576 | bytes 163840 | tf_op jit(solution)/shard_map/add | solution.py:234
  (1 shorter events, 0.0 us)
Async XLA Ops:
  0.6 32.5 %copy-start.1 = (bf16[512,256]{1,0:T(8,128)(2,1)S(1)}, bf16[512,256]{1,0:T(8,128)(2,1)}, u32[]{:S(2)}) copy-start(bf16[512,256]{1,0:T(8,128)(2,1)} %upstream.1) | copy-start | bytes 786436
  0.6 32.5 %copy-start = (bf16[1024,256]{1,0:T(8,128)(2,1)S(1)}, bf16[1024,256]{1,0:T(8,128)(2,1)}, u32[]{:S(2)}) copy-start(bf16[1024,256]{1,0:T(8,128)(2,1)} %weight.1) | copy-start | bytes 1572868
  33.9 1.6 %collective-permute-start = (bf16[16,32,256]{2,1,0:T(8,128)(2,1)S(1)}, bf16[16,32,256]{2,1,0:T(8,128)(2,1)S(1)}, u32[]{:S(2)}, u32[]{:S(2)}) collective-permute-start(bf16[16,32,256]{2,1,0:T(8,128)(2,1)S(1)} %get-tuple-element.11), channel_id=1, source_target_pairs={{0,1},{1,0},{2,3},{3,2},{4,5},{5,4},{6,7},{7,6},{8,9},{9,8},{10,11... | collective-permute-start | bytes 786440 | tf_op jit(solution)/shard_map/ppermute | solution.py:208
  48.1 4.7 %collective-permute-start.3 = (f32[32,256]{1,0:T(8,128)S(1)}, f32[32,256]{1,0:T(8,128)S(1)}, u32[]{:S(2)}, u32[]{:S(2)}) collective-permute-start(f32[32,256]{1,0:T(8,128)S(1)} %convert_reduce_fusion), channel_id=1, source_target_pairs={{0,96},{32,0},{64,32},{96,64},{1,97},{33,1},{65,33},{97,65},{2,98}... | collective-permute-start | bytes 98312 | tf_op jit(solution)/shard_map/ppermute | solution.py:234
  51.2 5.4 %collective-permute-start.2 = (f32[32,256]{1,0:T(8,128)S(1)}, f32[32,256]{1,0:T(8,128)S(1)}, u32[]{:S(2)}, u32[]{:S(2)}) collective-permute-start(f32[32,256]{1,0:T(8,128)S(1)} %convert_reduce_fusion), channel_id=1, source_target_pairs={{0,64},{32,96},{64,0},{96,32},{1,65},{33,97},{65,1},{97,33},{2,66}... | collective-permute-start | bytes 98312 | tf_op jit(solution)/shard_map/ppermute | solution.py:234
  51.8 5.1 %collective-permute-start.1 = (f32[32,256]{1,0:T(8,128)S(1)}, f32[32,256]{1,0:T(8,128)S(1)}, u32[]{:S(2)}, u32[]{:S(2)}) collective-permute-start(f32[32,256]{1,0:T(8,128)S(1)} %convert_reduce_fusion), channel_id=1, source_target_pairs={{0,32},{32,64},{64,96},{96,0},{1,33},{33,65},{65,97},{97,1},{2,34}... | collective-permute-start | bytes 98312 | tf_op jit(solution)/shard_map/ppermute | solution.py:234

commit v4 on v3

--- a/solution.py
+++ b/solution.py
@@ -13,7 +13,7 @@
 TILE = 128
 CHUNK = 32
 AHEAD = 3
-FINISH = 16
+FINISH = 8
 
 
 def aggregate_kernel(
@@ -51,7 +51,11 @@
 
     fetch_rows = pltpu.make_async_copy(row_index, rows, index_sem.at[0])
     fetch_cols = pltpu.make_async_copy(col_index, cols, index_sem.at[1])
-    fetch_own = pltpu.make_async_copy(features.at[:, pl.ds(0, NT)], own, self_sem)
+
+    def own_copy(part):
+        span = pl.ds(part * (FINISH * block), FINISH * block)
+        return pltpu.make_async_copy(features.at[:, span], own.at[:, span], self_sem.at[part])
+
     fetch_cols.start()
     fetch_rows.start()
     mask_copy(0).start()
@@ -97,16 +101,16 @@
     def _(chunk):
         chunk_step(chunk, True)
 
-    fetch_own.start()
+    for part in range(peers // FINISH):
+        own_copy(part).start()
 
     @pl.loop(chunks - AHEAD, chunks)
     def _(chunk):
         chunk_step(chunk, False)
 
-    fetch_own.wait()
-
     @pl.loop(0, peers // FINISH)
     def _(step):
+        own_copy(step).wait()
         for k in range(FINISH):
             peer = step * FINISH + k
             span = pl.ds(pl.multiple_of(peer * block, block), block)
@@ -138,7 +142,7 @@
             pltpu.VMEM((tiles, feat_cols, TILE), jnp.float32),
             pltpu.VMEM((tiles, TILE, TILE), jnp.int32),
             pltpu.SemaphoreType.DMA((2,)),
-            pltpu.SemaphoreType.DMA,
+            pltpu.SemaphoreType.DMA((peers // FINISH,)),
             pltpu.SemaphoreType.DMA((chunks,)),
             pltpu.SemaphoreType.DMA((chunks,)),
         ],
@@ -223,15 +227,16 @@
 def per_device(features, tile_rows, tile_cols, tile_masks, weight, upstream):
     peers = weight.shape[0] // features.shape[0]
     hidden = aggregate(features, tile_rows, tile_cols, tile_masks, peers)
+    hidden, weight, upstream = lax.optimization_barrier((hidden, weight, upstream))
     hidden = lax.all_to_all(hidden, FEAT, 0, 0)
     hidden = hidden.reshape(peers // CORES, CORES, *hidden.shape[1:])
     activation, partial = layer(hidden, weight, upstream)
     partial = lax.all_to_all(partial, ("z", "x"), 0, 0)
     local_grad = jnp.sum(partial.astype(jnp.float32), axis=0)
     weight_grad = local_grad
-    for shift in range(1, N_MB):
-        ring = [(member, (member + shift) % N_MB) for member in range(N_MB)]
-        weight_grad += lax.ppermute(local_grad, "mb", ring)
+    for shift in (1, 3, 2):
+        pairs = [(member, member ^ shift) for member in range(N_MB)]
+        weight_grad += lax.ppermute(local_grad, "mb", pairs)
     return (activation, weight_grad)
 
 

time: 57.7 us -> 57.1 us (0.990)
  no operation moved by 1% of the time
where the time goes in v4:
time: 57.1 us; the launch traced here: 56.9 us
  blocking collectives  37.7 us (66%)
  Pallas kernels  8.89 us (16%)
  starting transfers between devices  4.52 us (8%)
  waiting for transfers between devices  4.39 us (8%)
  other arithmetic  0.74 us (1%)
  between operations  0.67 us (1%)
    all_to_all x1, blocking collectives, per_device(): hidden = lax.all_to_all(hidden, FEAT, 0, 0)  25.3 us
    all_to_all x1, blocking collectives, per_device(): partial = lax.all_to_all(partial, ('z', 'x'), 0, 0)  12.4 us
    pallas_call x1, Pallas kernels, aggregate(): pl.pallas_call(aggregate_kernel, out_shape=jax.ShapeDtypeStruct((peers, f...  6.97 us
    ppermute x3, starting transfers between devices, per_device(): weight_grad += lax.ppermute(local_grad, 'mb', pairs)  4.33 us
    ppermute x3, waiting for transfers between devices, per_device(): weight_grad += lax.ppermute(local_grad, 'mb', pairs)  4.07 us
    pallas_call x2, Pallas kernels, call_in_vmem(): pl.pallas_call(kernel, out_shape=outputs, in_specs=[in_vmem] * len(operan...  1.92 us
  transfers between devices with their start and end apart: 4, of which 3 were waited for; matrix products, arithmetic and copies ran while one was open for 0% of the time, Pallas kernels for 2%

profile of v4, /device:TPU:0, one launch (start us, length us, event | category | flops | bytes accessed | tf_op | source)
XLA Modules:
  0.0 56.9 jit_solution(17129930968970239751)
XLA Ops:
  0.6 0.0 copy-start.1
  0.6 0.0 copy-start
  0.7 7.0 %aggregate.1 = bf16[32,32,512]{2,1,0:T(8,128)(2,1)S(1)} custom-call(s32[192]{0:T(256)} %row_index.1, s32[192]{0:T(256)} %col_index.1, f32[32,65536]{1,0:T(8,128)} %features.1, s32[192,128,128]{2,1,0:T(8,128)} %masks.1), custom_call_target="tpu_custom_call" | custom-call | tf_op jit(solution)/shard_map/aggregate/pallas_call | solution.py:126
  7.6 25.3 %all_to_all.10 = bf16[32,32,512]{2,1,0:T(8,128)(2,1)S(1)} all-to-all(bf16[32,32,512]{2,1,0:T(8,128)(2,1)S(1)} %aggregate.1), channel_id=1, replica_groups=mesh['mb'=4,'z'=4,'x'=4,'core'=2] {'z','x','core'}, dimensions={0} | all-to-all | bytes 2097152 | tf_op jit(solution)/shard_map/all_to_all | solution.py:231
  32.9 0.0 copy-done.1
  32.9 0.0 copy-done
  32.9 0.8 %slopes.1 = (f32[512,256]{1,0:T(8,128)S(1)}, bf16[512,256]{1,0:T(8,128)(2,1)S(1)}, bf16[16,32,256]{2,1,0:T(8,128)(2,1)S(1)}) custom-call(bf16[16,2,32,512]{3,2,1,0:T(8,128)(2,1)S(1)} %bitcast.1, bf16[1024,256]{1,0:T(8,128)(2,1)S(1)} %copy-done, bf16[512,256]{1,0:T(8,128)(2,1)S(1)} %copy-done.1), custom_call_target="tpu_custom_call" | custom-call | tf_op jit(solution)/shard_map/slopes/pallas_call | solution.py:187
  33.7 0.2 collective-permute-start
  33.9 1.1 %rest.1 = (bf16[512,256]{1,0:T(8,128)(2,1)}, f32[16,32,256]{2,1,0:T(8,128)S(1)}) custom-call(bf16[16,2,32,512]{3,2,1,0:T(8,128)(2,1)S(1)} %bitcast.2, f32[512,256]{1,0:T(8,128)S(1)} %get-tuple-element.13.preact, bf16[512,256]{1,0:T(8,128)(2,1)S(1)} %get-tuple-element.14.slopes), custom_call_target="tpu_custom_call" | custom-call | tf_op jit(solution)/shard_map/rest/pallas_call | solution.py:187
  35.0 0.3 collective-permute-done
  35.4 0.1 add_convert_fusion
  35.4 12.4 %all_to_all.11 = bf16[16,32,256]{2,1,0:T(8,128)(2,1)S(1)} all-to-all(bf16[16,32,256]{2,1,0:T(8,128)(2,1)S(1)} %add_convert_fusion), channel_id=1, replica_groups=mesh['mb'=4,'z'=4,'x'=4,'core'=2] {'z','x'}, dimensions={0} | all-to-all | bytes 524288 | tf_op jit(solution)/shard_map/all_to_all | solution.py:234
  47.9 3.3 %collective-permute-start.3 = (f32[32,256]{1,0:T(8,128)S(1)}, f32[32,256]{1,0:T(8,128)S(1)}, u32[]{:S(2)}, u32[]{:S(2)}) collective-permute-start(f32[32,256]{1,0:T(8,128)S(1)} %convert_reduce_fusion), channel_id=1, source_target_pairs={{0,64},{32,96},{64,0},{96,32},{1,65},{33,97},{65,1},{97,33},{2,66}... | collective-permute-start | bytes 98312 | tf_op jit(solution)/shard_map/ppermute | solution.py:239
  51.2 1.1 %collective-permute-start.2 = (f32[32,256]{1,0:T(8,128)S(1)}, f32[32,256]{1,0:T(8,128)S(1)}, u32[]{:S(2)}, u32[]{:S(2)}) collective-permute-start(f32[32,256]{1,0:T(8,128)S(1)} %convert_reduce_fusion), channel_id=1, source_target_pairs={{0,96},{32,64},{64,32},{96,0},{1,97},{33,65},{65,33},{97,1},{2,98}... | collective-permute-start | bytes 98312 | tf_op jit(solution)/shard_map/ppermute | solution.py:239
  52.2 0.0 collective-permute-start.1
  52.2 1.2 %collective-permute-done.3 = f32[32,256]{1,0:T(8,128)S(1)} collective-permute-done((f32[32,256]{1,0:T(8,128)S(1)}, f32[32,256]{1,0:T(8,128)S(1)}, u32[]{:S(2)}, u32[]{:S(2)}) %collective-permute-start.3) | collective-permute-done | bytes 32800 | tf_op jit(solution)/shard_map/ppermute | solution.py:239
  53.4 2.9 %collective-permute-done.2 = f32[32,256]{1,0:T(8,128)S(1)} collective-permute-done((f32[32,256]{1,0:T(8,128)S(1)}, f32[32,256]{1,0:T(8,128)S(1)}, u32[]{:S(2)}, u32[]{:S(2)}) %collective-permute-start.2) | collective-permute-done | bytes 32800 | tf_op jit(solution)/shard_map/ppermute | solution.py:239
  56.3 0.0 collective-permute-done.1
  56.3 0.6 %add_add_fusion = f32[32,256]{1,0:T(8,128)} fusion(f32[32,256]{1,0:T(8,128)S(1)} %collective-permute-done.3, f32[32,256]{1,0:T(8,128)S(1)} %collective-permute-done.2, f32[32,256]{1,0:T(8,128)S(1)} %convert_reduce_fusion, f32[32,256]{1,0:T(8,128)S(1)} %collective-permute-done.1), kind=kLoop, calls=%fused_computation.2 | loop fusion | flops 24576 | bytes 163840 | tf_op jit(solution)/shard_map/add | solution.py:239
  (1 shorter events, 0.0 us)
Async XLA Ops:
  0.6 32.3 %copy-start.1 = (bf16[512,256]{1,0:T(8,128)(2,1)S(1)}, bf16[512,256]{1,0:T(8,128)(2,1)}, u32[]{:S(2)}) copy-start(bf16[512,256]{1,0:T(8,128)(2,1)} %upstream) | copy-start | bytes 786436
  0.6 32.3 %copy-start = (bf16[1024,256]{1,0:T(8,128)(2,1)S(1)}, bf16[1024,256]{1,0:T(8,128)(2,1)}, u32[]{:S(2)}) copy-start(bf16[1024,256]{1,0:T(8,128)(2,1)} %weight) | copy-start | bytes 1572868
  33.7 1.6 %collective-permute-start = (bf16[16,32,256]{2,1,0:T(8,128)(2,1)S(1)}, bf16[16,32,256]{2,1,0:T(8,128)(2,1)S(1)}, u32[]{:S(2)}, u32[]{:S(2)}) collective-permute-start(bf16[16,32,256]{2,1,0:T(8,128)(2,1)S(1)} %get-tuple-element.17), channel_id=1, source_target_pairs={{0,1},{1,0},{2,3},{3,2},{4,5},{5,4},{6,7},{7,6},{8,9},{9,8},{10,11... | collective-permute-start | bytes 786440 | tf_op jit(solution)/shard_map/ppermute | solution.py:212
  47.9 5.5 %collective-permute-start.3 = (f32[32,256]{1,0:T(8,128)S(1)}, f32[32,256]{1,0:T(8,128)S(1)}, u32[]{:S(2)}, u32[]{:S(2)}) collective-permute-start(f32[32,256]{1,0:T(8,128)S(1)} %convert_reduce_fusion), channel_id=1, source_target_pairs={{0,64},{32,96},{64,0},{96,32},{1,65},{33,97},{65,1},{97,33},{2,66}... | collective-permute-start | bytes 98312 | tf_op jit(solution)/shard_map/ppermute | solution.py:239
  51.2 5.1 %collective-permute-start.2 = (f32[32,256]{1,0:T(8,128)S(1)}, f32[32,256]{1,0:T(8,128)S(1)}, u32[]{:S(2)}, u32[]{:S(2)}) collective-permute-start(f32[32,256]{1,0:T(8,128)S(1)} %convert_reduce_fusion), channel_id=1, source_target_pairs={{0,96},{32,64},{64,32},{96,0},{1,97},{33,65},{65,33},{97,1},{2,98}... | collective-permute-start | bytes 98312 | tf_op jit(solution)/shard_map/ppermute | solution.py:239
  52.2 4.1 %collective-permute-start.1 = (f32[32,256]{1,0:T(8,128)S(1)}, f32[32,256]{1,0:T(8,128)S(1)}, u32[]{:S(2)}, u32[]{:S(2)}) collective-permute-start(f32[32,256]{1,0:T(8,128)S(1)} %convert_reduce_fusion), channel_id=1, source_target_pairs={{0,32},{32,0},{64,96},{96,64},{1,33},{33,1},{65,97},{97,65},{2,34}... | collective-permute-start | bytes 98312 | tf_op jit(solution)/shard_map/ppermute | solution.py:239

commit v5 on v4

--- a/solution.py
+++ b/solution.py
@@ -7,13 +7,14 @@
 from jax.sharding import PartitionSpec as P
 
 NT = 16384
-N_MB = 4
+MB_TARGETS = ((1, 0, 3, 2), (2, 3, 1, 0), (3, 2, 0, 1))
 CORES = 2
 FEAT = ("z", "x", "core")
 TILE = 128
 CHUNK = 32
 AHEAD = 3
 FINISH = 8
+SPAN = 256
 
 
 def aggregate_kernel(
@@ -162,15 +163,20 @@
 
 def slopes_kernel(hidden, weight, upstream, preact, slopes, sent):
     chips, cores, feat_cols, block = hidden.shape
-    for first in range(0, block, TILE):
-        span = slice(first, first + TILE)
-        features = hidden[:, :, :, span].reshape(chips * cores * feat_cols, TILE)
-        value = jnp.dot(features.T, weight[...], preferred_element_type=jnp.float32)
-        preact[span] = value
-        slope = gate(value) + value * jnp.exp(-0.5 * value * value) * 0.3989422804014327
-        slopes[span] = (upstream[span].astype(jnp.float32) * slope).astype(jnp.bfloat16)
-    rows = hidden[:, 1 - lax.axis_index("core")].reshape(chips * feat_cols, block)
-    grad = jnp.dot(rows, slopes[...], preferred_element_type=jnp.float32)
+    other = 1 - lax.axis_index("core")
+    grad = None
+    for first in range(0, block, SPAN):
+        span = slice(first, first + SPAN)
+        for begin in range(first, first + SPAN, TILE):
+            part = slice(begin, begin + TILE)
+            features = hidden[:, :, :, part].reshape(chips * cores * feat_cols, TILE)
+            value = jnp.dot(features.T, weight[...], preferred_element_type=jnp.float32)
+            preact[part] = value
+            slope = gate(value) + value * jnp.exp(-0.5 * value * value) * 0.3989422804014327
+            slopes[part] = (upstream[part].astype(jnp.float32) * slope).astype(jnp.bfloat16)
+        rows = hidden[:, other, :, span].reshape(chips * feat_cols, SPAN)
+        term = jnp.dot(rows, slopes[span], preferred_element_type=jnp.float32)
+        grad = term if grad is None else grad + term
     sent[...] = grad.astype(jnp.bfloat16).reshape(sent.shape)
 
 
@@ -227,15 +233,14 @@
 def per_device(features, tile_rows, tile_cols, tile_masks, weight, upstream):
     peers = weight.shape[0] // features.shape[0]
     hidden = aggregate(features, tile_rows, tile_cols, tile_masks, peers)
-    hidden, weight, upstream = lax.optimization_barrier((hidden, weight, upstream))
     hidden = lax.all_to_all(hidden, FEAT, 0, 0)
     hidden = hidden.reshape(peers // CORES, CORES, *hidden.shape[1:])
     activation, partial = layer(hidden, weight, upstream)
     partial = lax.all_to_all(partial, ("z", "x"), 0, 0)
     local_grad = jnp.sum(partial.astype(jnp.float32), axis=0)
     weight_grad = local_grad
-    for shift in (1, 3, 2):
-        pairs = [(member, member ^ shift) for member in range(N_MB)]
+    for targets in MB_TARGETS:
+        pairs = list(enumerate(targets))
         weight_grad += lax.ppermute(local_grad, "mb", pairs)
     return (activation, weight_grad)
 

time: 57.1 us -> 56.9 us (level)
  waiting for transfers between devices: 4.39 us -> 3.36 us
  starting transfers between devices: 4.52 us -> 5.37 us
    ppermute x3, waiting for transfers between devices: 4.07 us -> 3.04 us  [per_device(): weight_grad += lax.ppermute(local_grad, 'mb', pairs)]
    ppermute x3, starting transfers between devices: 4.33 us -> 5.17 us  [per_device(): weight_grad += lax.ppermute(local_grad, 'mb', pairs)]
where the time goes in v5:
time: 56.9 us; the launch traced here: 56.7 us
  blocking collectives  37.7 us (66%)
  Pallas kernels  8.88 us (16%)
  starting transfers between devices  5.37 us (9%)
  waiting for transfers between devices  3.36 us (6%)
  other arithmetic  0.74 us (1%)
  between operations  0.67 us (1%)
    all_to_all x1, blocking collectives, per_device(): hidden = lax.all_to_all(hidden, FEAT, 0, 0)  25.3 us
    all_to_all x1, blocking collectives, per_device(): partial = lax.all_to_all(partial, ('z', 'x'), 0, 0)  12.4 us
    pallas_call x1, Pallas kernels, aggregate(): pl.pallas_call(aggregate_kernel, out_shape=jax.ShapeDtypeStruct((peers, f...  6.97 us
    ppermute x3, starting transfers between devices, per_device(): weight_grad += lax.ppermute(local_grad, 'mb', pairs)  5.17 us
    ppermute x3, waiting for transfers between devices, per_device(): weight_grad += lax.ppermute(local_grad, 'mb', pairs)  3.04 us
    pallas_call x2, Pallas kernels, call_in_vmem(): pl.pallas_call(kernel, out_shape=outputs, in_specs=[in_vmem] * len(operan...  1.91 us
  transfers between devices with their start and end apart: 4, of which 3 were waited for; matrix products, arithmetic and copies ran while one was open for 0% of the time, Pallas kernels for 2%

profile of v5, /device:TPU:0, one launch (start us, length us, event | category | flops | bytes accessed | tf_op | source)
XLA Modules:
  0.0 56.7 jit_solution(15854592927175421384)
XLA Ops:
  0.6 0.0 copy-start.1
  0.6 0.0 copy-start
  0.7 7.0 %aggregate.1 = bf16[32,32,512]{2,1,0:T(8,128)(2,1)S(1)} custom-call(s32[192]{0:T(256)} %row_index.1, s32[192]{0:T(256)} %col_index.1, f32[32,65536]{1,0:T(8,128)} %features.1, s32[192,128,128]{2,1,0:T(8,128)} %masks.1), custom_call_target="tpu_custom_call" | custom-call | tf_op jit(solution)/shard_map/aggregate/pallas_call | solution.py:127
  7.6 25.3 %all_to_all.10 = bf16[32,32,512]{2,1,0:T(8,128)(2,1)S(1)} all-to-all(bf16[32,32,512]{2,1,0:T(8,128)(2,1)S(1)} %aggregate.1), channel_id=1, replica_groups=mesh['mb'=4,'z'=4,'x'=4,'core'=2] {'z','x','core'}, dimensions={0} | all-to-all | bytes 2097152 | tf_op jit(solution)/shard_map/all_to_all | solution.py:236
  32.9 0.0 copy-done.1
  32.9 0.0 copy-done
  32.9 0.8 %slopes.1 = (f32[512,256]{1,0:T(8,128)S(1)}, bf16[512,256]{1,0:T(8,128)(2,1)S(1)}, bf16[16,32,256]{2,1,0:T(8,128)(2,1)S(1)}) custom-call(bf16[16,2,32,512]{3,2,1,0:T(8,128)(2,1)S(1)} %bitcast.1, bf16[1024,256]{1,0:T(8,128)(2,1)S(1)} %copy-done, bf16[512,256]{1,0:T(8,128)(2,1)S(1)} %copy-done.1), custom_call_target="tpu_custom_call" | custom-call | tf_op jit(solution)/shard_map/slopes/pallas_call | solution.py:193
  33.7 0.2 collective-permute-start
  33.9 1.1 %rest.1 = (bf16[512,256]{1,0:T(8,128)(2,1)}, f32[16,32,256]{2,1,0:T(8,128)S(1)}) custom-call(bf16[16,2,32,512]{3,2,1,0:T(8,128)(2,1)S(1)} %bitcast.2, f32[512,256]{1,0:T(8,128)S(1)} %get-tuple-element.7.preact, bf16[512,256]{1,0:T(8,128)(2,1)S(1)} %get-tuple-element.8.slopes), custom_call_target="tpu_custom_call" | custom-call | tf_op jit(solution)/shard_map/rest/pallas_call | solution.py:193
  35.0 0.3 collective-permute-done
  35.4 0.1 add_convert_fusion
  35.4 12.4 %all_to_all.11 = bf16[16,32,256]{2,1,0:T(8,128)(2,1)S(1)} all-to-all(bf16[16,32,256]{2,1,0:T(8,128)(2,1)S(1)} %add_convert_fusion), channel_id=1, replica_groups=mesh['mb'=4,'z'=4,'x'=4,'core'=2] {'z','x'}, dimensions={0} | all-to-all | bytes 524288 | tf_op jit(solution)/shard_map/all_to_all | solution.py:239
  47.9 3.1 %collective-permute-start.3 = (f32[32,256]{1,0:T(8,128)S(1)}, f32[32,256]{1,0:T(8,128)S(1)}, u32[]{:S(2)}, u32[]{:S(2)}) collective-permute-start(f32[32,256]{1,0:T(8,128)S(1)} %convert_reduce_fusion), channel_id=1, source_target_pairs={{0,96},{32,64},{64,0},{96,32},{1,97},{33,65},{65,1},{97,33},{2,98}... | collective-permute-start | bytes 98312 | tf_op jit(solution)/shard_map/ppermute | solution.py:244
  51.0 0.5 collective-permute-start.2
  51.5 1.6 %collective-permute-start.1 = (f32[32,256]{1,0:T(8,128)S(1)}, f32[32,256]{1,0:T(8,128)S(1)}, u32[]{:S(2)}, u32[]{:S(2)}) collective-permute-start(f32[32,256]{1,0:T(8,128)S(1)} %convert_reduce_fusion), channel_id=1, source_target_pairs={{0,32},{32,0},{64,96},{96,64},{1,33},{33,1},{65,97},{97,65},{2,34}... | collective-permute-start | bytes 98312 | tf_op jit(solution)/shard_map/ppermute | solution.py:244
  53.1 0.3 collective-permute-done.3
  53.4 2.7 %collective-permute-done.2 = f32[32,256]{1,0:T(8,128)S(1)} collective-permute-done((f32[32,256]{1,0:T(8,128)S(1)}, f32[32,256]{1,0:T(8,128)S(1)}, u32[]{:S(2)}, u32[]{:S(2)}) %collective-permute-start.2) | collective-permute-done | bytes 32800 | tf_op jit(solution)/shard_map/ppermute | solution.py:244
  56.1 0.0 collective-permute-done.1
  56.1 0.6 %add_add_fusion = f32[32,256]{1,0:T(8,128)} fusion(f32[32,256]{1,0:T(8,128)S(1)} %collective-permute-done.3, f32[32,256]{1,0:T(8,128)S(1)} %collective-permute-done.2, f32[32,256]{1,0:T(8,128)S(1)} %convert_reduce_fusion, f32[32,256]{1,0:T(8,128)S(1)} %collective-permute-done.1), kind=kLoop, calls=%fused_computation.2 | loop fusion | flops 24576 | bytes 163840 | tf_op jit(solution)/shard_map/add | solution.py:244
  (1 shorter events, 0.0 us)
Async XLA Ops:
  0.6 32.3 %copy-start.1 = (bf16[512,256]{1,0:T(8,128)(2,1)S(1)}, bf16[512,256]{1,0:T(8,128)(2,1)}, u32[]{:S(2)}) copy-start(bf16[512,256]{1,0:T(8,128)(2,1)} %upstream.1) | copy-start | bytes 786436
  0.6 32.3 %copy-start = (bf16[1024,256]{1,0:T(8,128)(2,1)S(1)}, bf16[1024,256]{1,0:T(8,128)(2,1)}, u32[]{:S(2)}) copy-start(bf16[1024,256]{1,0:T(8,128)(2,1)} %weight.1) | copy-start | bytes 1572868
  33.7 1.6 %collective-permute-start = (bf16[16,32,256]{2,1,0:T(8,128)(2,1)S(1)}, bf16[16,32,256]{2,1,0:T(8,128)(2,1)S(1)}, u32[]{:S(2)}, u32[]{:S(2)}) collective-permute-start(bf16[16,32,256]{2,1,0:T(8,128)(2,1)S(1)} %get-tuple-element.11), channel_id=1, source_target_pairs={{0,1},{1,0},{2,3},{3,2},{4,5},{5,4},{6,7},{7,6},{8,9},{9,8},{10,11... | collective-permute-start | bytes 786440 | tf_op jit(solution)/shard_map/ppermute | solution.py:218
  47.9 5.5 %collective-permute-start.3 = (f32[32,256]{1,0:T(8,128)S(1)}, f32[32,256]{1,0:T(8,128)S(1)}, u32[]{:S(2)}, u32[]{:S(2)}) collective-permute-start(f32[32,256]{1,0:T(8,128)S(1)} %convert_reduce_fusion), channel_id=1, source_target_pairs={{0,96},{32,64},{64,0},{96,32},{1,97},{33,65},{65,1},{97,33},{2,98}... | collective-permute-start | bytes 98312 | tf_op jit(solution)/shard_map/ppermute | solution.py:244
  51.0 5.1 %collective-permute-start.2 = (f32[32,256]{1,0:T(8,128)S(1)}, f32[32,256]{1,0:T(8,128)S(1)}, u32[]{:S(2)}, u32[]{:S(2)}) collective-permute-start(f32[32,256]{1,0:T(8,128)S(1)} %convert_reduce_fusion), channel_id=1, source_target_pairs={{0,64},{32,96},{64,32},{96,0},{1,65},{33,97},{65,33},{97,1},{2,66}... | collective-permute-start | bytes 98312 | tf_op jit(solution)/shard_map/ppermute | solution.py:244
  51.5 4.6 %collective-permute-start.1 = (f32[32,256]{1,0:T(8,128)S(1)}, f32[32,256]{1,0:T(8,128)S(1)}, u32[]{:S(2)}, u32[]{:S(2)}) collective-permute-start(f32[32,256]{1,0:T(8,128)S(1)} %convert_reduce_fusion), channel_id=1, source_target_pairs={{0,32},{32,0},{64,96},{96,64},{1,33},{33,1},{65,97},{97,65},{2,34}... | collective-permute-start | bytes 98312 | tf_op jit(solution)/shard_map/ppermute | solution.py:244

commit v6 on v5

--- a/solution.py
+++ b/solution.py
@@ -180,11 +180,14 @@
     sent[...] = grad.astype(jnp.bfloat16).reshape(sent.shape)
 
 
-def rest_kernel(hidden, preact, slopes, activation, kept):
+def kept_kernel(hidden, slopes, kept):
     chips, cores, feat_cols, block = hidden.shape
     rows = hidden[:, lax.axis_index("core")].reshape(chips * feat_cols, block)
     grad = jnp.dot(rows, slopes[...], preferred_element_type=jnp.float32)
     kept[...] = grad.reshape(kept.shape)
+
+
+def activation_kernel(preact, activation):
     activation[...] = (preact[...] * gate(preact[...])).astype(jnp.bfloat16)
 
 
@@ -216,18 +219,10 @@
         upstream,
     )
     received = lax.ppermute(sent, "core", [(0, 1), (1, 0)])
-    activation, kept = call_in_vmem(
-        rest_kernel,
-        "rest",
-        (
-            jax.ShapeDtypeStruct(upstream.shape, jnp.bfloat16),
-            jax.ShapeDtypeStruct(grad_shape, jnp.float32),
-        ),
-        hidden,
-        preact,
-        slopes,
-    )
-    return activation, (kept + received).astype(jnp.bfloat16)
+    (kept,) = call_in_vmem(
+        kept_kernel, "kept", (jax.ShapeDtypeStruct(grad_shape, jnp.float32),), hidden, slopes
+    )
+    return preact, (kept + received).astype(jnp.bfloat16)
 
 
 def per_device(features, tile_rows, tile_cols, tile_masks, weight, upstream):
@@ -235,9 +230,16 @@
     hidden = aggregate(features, tile_rows, tile_cols, tile_masks, peers)
     hidden = lax.all_to_all(hidden, FEAT, 0, 0)
     hidden = hidden.reshape(peers // CORES, CORES, *hidden.shape[1:])
-    activation, partial = layer(hidden, weight, upstream)
+    preact, partial = layer(hidden, weight, upstream)
     partial = lax.all_to_all(partial, ("z", "x"), 0, 0)
     local_grad = jnp.sum(partial.astype(jnp.float32), axis=0)
+    local_grad, preact = lax.optimization_barrier((local_grad, preact))
+    (activation,) = call_in_vmem(
+        activation_kernel,
+        "activation",
+        (jax.ShapeDtypeStruct(preact.shape, jnp.bfloat16),),
+        preact,
+    )
     weight_grad = local_grad
     for targets in MB_TARGETS:
         pairs = list(enumerate(targets))

time: 56.9 us -> 56.9 us (level)
    ppermute x3, waiting for transfers between devices: 3.04 us -> 2.22 us  [per_device(): weight_grad += lax.ppermute(local_grad, 'mb', pairs)]
    ppermute x1, waiting for transfers between devices: 0.33 us -> 1.12 us  [layer(): received = lax.ppermute(sent, 'core', [(0, 1), (1, 0)])]
    pallas_call x2 -> x3, Pallas kernels: 1.91 us -> 1.92 us  [call_in_vmem(): pl.pallas_call(kernel, out_shape=outputs, in_specs=[in_vmem] * len(operan...]
  transfers between devices with their start and end apart: 4 -> 4, of which waited for: 3 -> 2; matrix products, arithmetic and copies ran while one was open for 0% -> 0% of each run, Pallas kernels for 2% -> 2%
where the time goes in v6:
time: 56.9 us; the launch traced here: 56.7 us
  blocking collectives  37.7 us (66%)
  Pallas kernels  8.89 us (16%)
  starting transfers between devices  5.36 us (9%)
  waiting for transfers between devices  3.35 us (6%)
  other arithmetic  0.74 us (1%)
  between operations  0.68 us (1%)
    all_to_all x1, blocking collectives, per_device(): hidden = lax.all_to_all(hidden, FEAT, 0, 0)  25.3 us
    all_to_all x1, blocking collectives, per_device(): partial = lax.all_to_all(partial, ('z', 'x'), 0, 0)  12.4 us
    pallas_call x1, Pallas kernels, aggregate(): pl.pallas_call(aggregate_kernel, out_shape=jax.ShapeDtypeStruct((peers, f...  6.97 us
    ppermute x3, starting transfers between devices, per_device(): weight_grad += lax.ppermute(local_grad, 'mb', pairs)  5.17 us
    ppermute x3, waiting for transfers between devices, per_device(): weight_grad += lax.ppermute(local_grad, 'mb', pairs)  2.22 us
    pallas_call x3, Pallas kernels, call_in_vmem(): pl.pallas_call(kernel, out_shape=outputs, in_specs=[in_vmem] * len(operan...  1.92 us
  transfers between devices with their start and end apart: 4, of which 2 were waited for; matrix products, arithmetic and copies ran while one was open for 0% of the time, Pallas kernels for 2%

profile of v6, /device:TPU:0, one launch (start us, length us, event | category | flops | bytes accessed | tf_op | source)
XLA Modules:
  0.0 56.7 jit_solution(4903069077837643256)
XLA Ops:
  0.6 0.0 copy-start.1
  0.6 0.0 copy-start
  0.7 7.0 %aggregate.1 = bf16[32,32,512]{2,1,0:T(8,128)(2,1)S(1)} custom-call(s32[192]{0:T(256)} %row_index.1, s32[192]{0:T(256)} %col_index.1, f32[32,65536]{1,0:T(8,128)} %features.1, s32[192,128,128]{2,1,0:T(8,128)} %masks.1), custom_call_target="tpu_custom_call" | custom-call | tf_op jit(solution)/shard_map/aggregate/pallas_call | solution.py:127
  7.6 25.3 %all_to_all.10 = bf16[32,32,512]{2,1,0:T(8,128)(2,1)S(1)} all-to-all(bf16[32,32,512]{2,1,0:T(8,128)(2,1)S(1)} %aggregate.1), channel_id=1, replica_groups=mesh['mb'=4,'z'=4,'x'=4,'core'=2] {'z','x','core'}, dimensions={0} | all-to-all | bytes 2097152 | tf_op jit(solution)/shard_map/all_to_all | solution.py:231
  32.9 0.0 copy-done.1
  32.9 0.0 copy-done
  32.9 0.8 %slopes.1 = (f32[512,256]{1,0:T(8,128)S(1)}, bf16[512,256]{1,0:T(8,128)(2,1)S(1)}, bf16[16,32,256]{2,1,0:T(8,128)(2,1)S(1)}) custom-call(bf16[16,2,32,512]{3,2,1,0:T(8,128)(2,1)S(1)} %bitcast.1, bf16[1024,256]{1,0:T(8,128)(2,1)S(1)} %copy-done, bf16[512,256]{1,0:T(8,128)(2,1)S(1)} %copy-done.1), custom_call_target="tpu_custom_call" | custom-call | tf_op jit(solution)/shard_map/slopes/pallas_call | solution.py:196
  33.7 0.2 collective-permute-start
  33.9 0.3 kept.1
  34.2 1.1 %collective-permute-done = bf16[16,32,256]{2,1,0:T(8,128)(2,1)S(1)} collective-permute-done((bf16[16,32,256]{2,1,0:T(8,128)(2,1)S(1)}, bf16[16,32,256]{2,1,0:T(8,128)(2,1)S(1)}, u32[]{:S(2)}, u32[]{:S(2)}) %collective-permute-start) | collective-permute-done | bytes 262176 | tf_op jit(solution)/shard_map/ppermute | solution.py:221
  35.4 0.1 add_convert_fusion
  35.4 12.4 %all_to_all.11 = bf16[16,32,256]{2,1,0:T(8,128)(2,1)S(1)} all-to-all(bf16[16,32,256]{2,1,0:T(8,128)(2,1)S(1)} %add_convert_fusion), channel_id=1, replica_groups=mesh['mb'=4,'z'=4,'x'=4,'core'=2] {'z','x'}, dimensions={0} | all-to-all | bytes 524288 | tf_op jit(solution)/shard_map/all_to_all | solution.py:234
  47.9 3.1 %collective-permute-start.3 = (f32[32,256]{1,0:T(8,128)S(1)}, f32[32,256]{1,0:T(8,128)S(1)}, u32[]{:S(2)}, u32[]{:S(2)}) collective-permute-start(f32[32,256]{1,0:T(8,128)S(1)} %convert_reduce_fusion), channel_id=1, source_target_pairs={{0,96},{32,64},{64,0},{96,32},{1,97},{33,65},{65,1},{97,33},{2,98}... | collective-permute-start | bytes 98312 | tf_op jit(solution)/shard_map/ppermute | solution.py:246
  51.0 0.5 collective-permute-start.2
  51.5 1.6 %collective-permute-start.1 = (f32[32,256]{1,0:T(8,128)S(1)}, f32[32,256]{1,0:T(8,128)S(1)}, u32[]{:S(2)}, u32[]{:S(2)}) collective-permute-start(f32[32,256]{1,0:T(8,128)S(1)} %convert_reduce_fusion), channel_id=1, source_target_pairs={{0,32},{32,0},{64,96},{96,64},{1,33},{33,1},{65,97},{97,65},{2,34}... | collective-permute-start | bytes 98312 | tf_op jit(solution)/shard_map/ppermute | solution.py:246
  53.1 0.8 %activation.1 = bf16[512,256]{1,0:T(8,128)(2,1)} custom-call(f32[512,256]{1,0:T(8,128)S(1)} %get-tuple-element.10.preact), custom_call_target="tpu_custom_call" | custom-call | tf_op jit(solution)/shard_map/activation/pallas_call | solution.py:196
  53.9 0.0 collective-permute-done.3
  53.9 2.2 %collective-permute-done.2 = f32[32,256]{1,0:T(8,128)S(1)} collective-permute-done((f32[32,256]{1,0:T(8,128)S(1)}, f32[32,256]{1,0:T(8,128)S(1)}, u32[]{:S(2)}, u32[]{:S(2)}) %collective-permute-start.2) | collective-permute-done | bytes 32800 | tf_op jit(solution)/shard_map/ppermute | solution.py:246
  56.1 0.0 collective-permute-done.1
  56.1 0.6 %add_add_fusion = f32[32,256]{1,0:T(8,128)} fusion(f32[32,256]{1,0:T(8,128)S(1)} %collective-permute-done.3, f32[32,256]{1,0:T(8,128)S(1)} %collective-permute-done.2, f32[32,256]{1,0:T(8,128)S(1)} %convert_reduce_fusion, f32[32,256]{1,0:T(8,128)S(1)} %collective-permute-done.1), kind=kLoop, calls=%fused_computation.2 | loop fusion | flops 24576 | bytes 163840 | tf_op jit(solution)/shard_map/add | solution.py:246
  (1 shorter events, 0.0 us)
Async XLA Ops:
  0.6 32.3 %copy-start.1 = (bf16[512,256]{1,0:T(8,128)(2,1)S(1)}, bf16[512,256]{1,0:T(8,128)(2,1)}, u32[]{:S(2)}) copy-start(bf16[512,256]{1,0:T(8,128)(2,1)} %upstream.1) | copy-start | bytes 786436
  0.6 32.3 %copy-start = (bf16[1024,256]{1,0:T(8,128)(2,1)S(1)}, bf16[1024,256]{1,0:T(8,128)(2,1)}, u32[]{:S(2)}) copy-start(bf16[1024,256]{1,0:T(8,128)(2,1)} %weight.1) | copy-start | bytes 1572868
  33.7 1.6 %collective-permute-start = (bf16[16,32,256]{2,1,0:T(8,128)(2,1)S(1)}, bf16[16,32,256]{2,1,0:T(8,128)(2,1)S(1)}, u32[]{:S(2)}, u32[]{:S(2)}) collective-permute-start(bf16[16,32,256]{2,1,0:T(8,128)(2,1)S(1)} %get-tuple-element.8), channel_id=1, source_target_pairs={{0,1},{1,0},{2,3},{3,2},{4,5},{5,4},{6,7},{7,6},{8,9},{9,8},{10,11... | collective-permute-start | bytes 786440 | tf_op jit(solution)/shard_map/ppermute | solution.py:221
  47.9 6.0 %collective-permute-start.3 = (f32[32,256]{1,0:T(8,128)S(1)}, f32[32,256]{1,0:T(8,128)S(1)}, u32[]{:S(2)}, u32[]{:S(2)}) collective-permute-start(f32[32,256]{1,0:T(8,128)S(1)} %convert_reduce_fusion), channel_id=1, source_target_pairs={{0,96},{32,64},{64,0},{96,32},{1,97},{33,65},{65,1},{97,33},{2,98}... | collective-permute-start | bytes 98312 | tf_op jit(solution)/shard_map/ppermute | solution.py:246
  51.0 5.1 %collective-permute-start.2 = (f32[32,256]{1,0:T(8,128)S(1)}, f32[32,256]{1,0:T(8,128)S(1)}, u32[]{:S(2)}, u32[]{:S(2)}) collective-permute-start(f32[32,256]{1,0:T(8,128)S(1)} %convert_reduce_fusion), channel_id=1, source_target_pairs={{0,64},{32,96},{64,32},{96,0},{1,65},{33,97},{65,33},{97,1},{2,66}... | collective-permute-start | bytes 98312 | tf_op jit(solution)/shard_map/ppermute | solution.py:246
  51.5 4.6 %collective-permute-start.1 = (f32[32,256]{1,0:T(8,128)S(1)}, f32[32,256]{1,0:T(8,128)S(1)}, u32[]{:S(2)}, u32[]{:S(2)}) collective-permute-start(f32[32,256]{1,0:T(8,128)S(1)} %convert_reduce_fusion), channel_id=1, source_target_pairs={{0,32},{32,0},{64,96},{96,64},{1,33},{33,1},{65,97},{97,65},{2,34}... | collective-permute-start | bytes 98312 | tf_op jit(solution)/shard_map/ppermute | solution.py:246

commit v7 on v6

--- a/solution.py
+++ b/solution.py
@@ -241,9 +241,10 @@
         preact,
     )
     weight_grad = local_grad
+    local_grad = local_grad.astype(jnp.bfloat16)
     for targets in MB_TARGETS:
         pairs = list(enumerate(targets))
-        weight_grad += lax.ppermute(local_grad, "mb", pairs)
+        weight_grad += lax.ppermute(local_grad, "mb", pairs).astype(jnp.float32)
     return (activation, weight_grad)
 
 

time: 56.9 us -> 56.7 us (level)
  no operation moved by 1% of the time
where the time goes in v7:
time: 56.7 us; the launch traced here: 56.6 us
  blocking collectives  37.7 us (66%)
  Pallas kernels  8.88 us (16%)
  starting transfers between devices  5.37 us (9%)
  waiting for transfers between devices  3.17 us (6%)
  other arithmetic  0.75 us (1%)
  between operations  0.69 us (1%)
    all_to_all x1, blocking collectives, per_device(): hidden = lax.all_to_all(hidden, FEAT, 0, 0)  25.3 us
    all_to_all x1, blocking collectives, per_device(): partial = lax.all_to_all(partial, ('z', 'x'), 0, 0)  12.4 us
    pallas_call x1, Pallas kernels, aggregate(): pl.pallas_call(aggregate_kernel, out_shape=jax.ShapeDtypeStruct((peers, f...  6.97 us
    ppermute x3, starting transfers between devices, per_device(): weight_grad += lax.ppermute(local_grad, 'mb', pairs).astype(jnp.float32)  5.18 us
    ppermute x3, waiting for transfers between devices, per_device(): weight_grad += lax.ppermute(local_grad, 'mb', pairs).astype(jnp.float32)  2.05 us
    pallas_call x3, Pallas kernels, call_in_vmem(): pl.pallas_call(kernel, out_shape=outputs, in_specs=[in_vmem] * len(operan...  1.91 us
  transfers between devices with their start and end apart: 4, of which 2 were waited for; matrix products, arithmetic and copies ran while one was open for 0% of the time, Pallas kernels for 2%

profile of v7, /device:TPU:0, one launch (start us, length us, event | category | flops | bytes accessed | tf_op | source)
XLA Modules:
  0.0 56.6 jit_solution(9389557164265874031)
XLA Ops:
  0.6 0.0 copy-start.1
  0.6 0.0 copy-start
  0.7 7.0 %aggregate.1 = bf16[32,32,512]{2,1,0:T(8,128)(2,1)S(1)} custom-call(s32[192]{0:T(256)} %row_index.1, s32[192]{0:T(256)} %col_index.1, f32[32,65536]{1,0:T(8,128)} %features.1, s32[192,128,128]{2,1,0:T(8,128)} %masks.1), custom_call_target="tpu_custom_call" | custom-call | tf_op jit(solution)/shard_map/aggregate/pallas_call | solution.py:127
  7.6 25.3 %all_to_all.10 = bf16[32,32,512]{2,1,0:T(8,128)(2,1)S(1)} all-to-all(bf16[32,32,512]{2,1,0:T(8,128)(2,1)S(1)} %aggregate.1), channel_id=1, replica_groups=mesh['mb'=4,'z'=4,'x'=4,'core'=2] {'z','x','core'}, dimensions={0} | all-to-all | bytes 2097152 | tf_op jit(solution)/shard_map/all_to_all | solution.py:231
  32.9 0.0 copy-done.1
  32.9 0.0 copy-done
  32.9 0.8 %slopes.1 = (f32[512,256]{1,0:T(8,128)S(1)}, bf16[512,256]{1,0:T(8,128)(2,1)S(1)}, bf16[16,32,256]{2,1,0:T(8,128)(2,1)S(1)}) custom-call(bf16[16,2,32,512]{3,2,1,0:T(8,128)(2,1)S(1)} %bitcast.1, bf16[1024,256]{1,0:T(8,128)(2,1)S(1)} %copy-done, bf16[512,256]{1,0:T(8,128)(2,1)S(1)} %copy-done.1), custom_call_target="tpu_custom_call" | custom-call | tf_op jit(solution)/shard_map/slopes/pallas_call | solution.py:196
  33.7 0.2 collective-permute-start
  33.9 0.3 kept.1
  34.2 1.1 %collective-permute-done = bf16[16,32,256]{2,1,0:T(8,128)(2,1)S(1)} collective-permute-done((bf16[16,32,256]{2,1,0:T(8,128)(2,1)S(1)}, bf16[16,32,256]{2,1,0:T(8,128)(2,1)S(1)}, u32[]{:S(2)}, u32[]{:S(2)}) %collective-permute-start) | collective-permute-done | bytes 262176 | tf_op jit(solution)/shard_map/ppermute | solution.py:221
  35.4 0.1 add_convert_fusion
  35.4 12.4 %all_to_all.11 = bf16[16,32,256]{2,1,0:T(8,128)(2,1)S(1)} all-to-all(bf16[16,32,256]{2,1,0:T(8,128)(2,1)S(1)} %add_convert_fusion), channel_id=1, replica_groups=mesh['mb'=4,'z'=4,'x'=4,'core'=2] {'z','x'}, dimensions={0} | all-to-all | bytes 524288 | tf_op jit(solution)/shard_map/all_to_all | solution.py:234
  47.9 3.1 %collective-permute-start.3 = (bf16[32,256]{1,0:T(8,128)(2,1)S(1)}, bf16[32,256]{1,0:T(8,128)(2,1)S(1)}, u32[]{:S(2)}, u32[]{:S(2)}) collective-permute-start(bf16[32,256]{1,0:T(8,128)(2,1)S(1)} %convert_element_type.24), channel_id=1, source_target_pairs={{0,96},{32,64},{64,0},{96,32},{1,97},{33,65},{65,1},{97,33},{2,98}... | collective-permute-start | bytes 49160 | tf_op jit(solution)/shard_map/ppermute | solution.py:247
  51.0 0.5 collective-permute-start.2
  51.5 1.6 %collective-permute-start.1 = (bf16[32,256]{1,0:T(8,128)(2,1)S(1)}, bf16[32,256]{1,0:T(8,128)(2,1)S(1)}, u32[]{:S(2)}, u32[]{:S(2)}) collective-permute-start(bf16[32,256]{1,0:T(8,128)(2,1)S(1)} %convert_element_type.24), channel_id=1, source_target_pairs={{0,32},{32,0},{64,96},{96,64},{1,33},{33,1},{65,97},{97,65},{2,34}... | collective-permute-start | bytes 49160 | tf_op jit(solution)/shard_map/ppermute | solution.py:247
  53.1 0.8 %activation.1 = bf16[512,256]{1,0:T(8,128)(2,1)} custom-call(f32[512,256]{1,0:T(8,128)S(1)} %get-tuple-element.10.preact), custom_call_target="tpu_custom_call" | custom-call | tf_op jit(solution)/shard_map/activation/pallas_call | solution.py:196
  53.9 0.0 collective-permute-done.3
  53.9 2.0 %collective-permute-done.2 = bf16[32,256]{1,0:T(8,128)(2,1)S(1)} collective-permute-done((bf16[32,256]{1,0:T(8,128)(2,1)S(1)}, bf16[32,256]{1,0:T(8,128)(2,1)S(1)}, u32[]{:S(2)}, u32[]{:S(2)}) %collective-permute-start.2) | collective-permute-done | bytes 16416 | tf_op jit(solution)/shard_map/ppermute | solution.py:247
  55.9 0.0 collective-permute-done.1
  55.9 0.6 %convert_add_fusion = f32[32,256]{1,0:T(8,128)} fusion(bf16[32,256]{1,0:T(8,128)(2,1)S(1)} %collective-permute-done.3, bf16[32,256]{1,0:T(8,128)(2,1)S(1)} %collective-permute-done.2, f32[32,256]{1,0:T(8,128)S(1)} %convert_reduce_fusion, bf16[32,256]{1,0:T(8,128)(2,1)S(1)} %collective-permute-done.1), kind=kLoop, calls=%fused_computation.2 | loop fusion | flops 49152 | bytes 114688 | tf_op jit(solution)/shard_map/add | solution.py:247
  (2 shorter events, 0.0 us)
Async XLA Ops:
  0.6 32.3 %copy-start.1 = (bf16[512,256]{1,0:T(8,128)(2,1)S(1)}, bf16[512,256]{1,0:T(8,128)(2,1)}, u32[]{:S(2)}) copy-start(bf16[512,256]{1,0:T(8,128)(2,1)} %upstream.1) | copy-start | bytes 786436
  0.6 32.3 %copy-start = (bf16[1024,256]{1,0:T(8,128)(2,1)S(1)}, bf16[1024,256]{1,0:T(8,128)(2,1)}, u32[]{:S(2)}) copy-start(bf16[1024,256]{1,0:T(8,128)(2,1)} %weight.1) | copy-start | bytes 1572868
  33.7 1.6 %collective-permute-start = (bf16[16,32,256]{2,1,0:T(8,128)(2,1)S(1)}, bf16[16,32,256]{2,1,0:T(8,128)(2,1)S(1)}, u32[]{:S(2)}, u32[]{:S(2)}) collective-permute-start(bf16[16,32,256]{2,1,0:T(8,128)(2,1)S(1)} %get-tuple-element.8), channel_id=1, source_target_pairs={{0,1},{1,0},{2,3},{3,2},{4,5},{5,4},{6,7},{7,6},{8,9},{9,8},{10,11... | collective-permute-start | bytes 786440 | tf_op jit(solution)/shard_map/ppermute | solution.py:221
  47.9 6.0 %collective-permute-start.3 = (bf16[32,256]{1,0:T(8,128)(2,1)S(1)}, bf16[32,256]{1,0:T(8,128)(2,1)S(1)}, u32[]{:S(2)}, u32[]{:S(2)}) collective-permute-start(bf16[32,256]{1,0:T(8,128)(2,1)S(1)} %convert_element_type.24), channel_id=1, source_target_pairs={{0,96},{32,64},{64,0},{96,32},{1,97},{33,65},{65,1},{97,33},{2,98}... | collective-permute-start | bytes 49160 | tf_op jit(solution)/shard_map/ppermute | solution.py:247
  51.0 4.9 %collective-permute-start.2 = (bf16[32,256]{1,0:T(8,128)(2,1)S(1)}, bf16[32,256]{1,0:T(8,128)(2,1)S(1)}, u32[]{:S(2)}, u32[]{:S(2)}) collective-permute-start(bf16[32,256]{1,0:T(8,128)(2,1)S(1)} %convert_element_type.24), channel_id=1, source_target_pairs={{0,64},{32,96},{64,32},{96,0},{1,65},{33,97},{65,33},{97,1},{2,66}... | collective-permute-start | bytes 49160 | tf_op jit(solution)/shard_map/ppermute | solution.py:247
  51.5 4.4 %collective-permute-start.1 = (bf16[32,256]{1,0:T(8,128)(2,1)S(1)}, bf16[32,256]{1,0:T(8,128)(2,1)S(1)}, u32[]{:S(2)}, u32[]{:S(2)}) collective-permute-start(bf16[32,256]{1,0:T(8,128)(2,1)S(1)} %convert_element_type.24), channel_id=1, source_target_pairs={{0,32},{32,0},{64,96},{96,64},{1,33},{33,1},{65,97},{97,65},{2,34}... | collective-permute-start | bytes 49160 | tf_op jit(solution)/shard_map/ppermute | solution.py:247

commit v8 on v7

--- a/solution.py
+++ b/solution.py
@@ -13,7 +13,7 @@
 TILE = 128
 CHUNK = 32
 AHEAD = 3
-FINISH = 8
+FINISH = 4
 SPAN = 256
 
 

time: 56.7 us -> 56.8 us (level)
  no operation moved by 1% of the time
where the time goes in v8:
time: 56.8 us; the launch traced here: 56.6 us
  blocking collectives  37.7 us (66%)
  Pallas kernels  8.96 us (16%)
  starting transfers between devices  5.37 us (9%)
  waiting for transfers between devices  3.17 us (6%)
  other arithmetic  0.75 us (1%)
  between operations  0.69 us (1%)
    all_to_all x1, blocking collectives, per_device(): hidden = lax.all_to_all(hidden, FEAT, 0, 0)  25.3 us
    all_to_all x1, blocking collectives, per_device(): partial = lax.all_to_all(partial, ('z', 'x'), 0, 0)  12.4 us
    pallas_call x1, Pallas kernels, aggregate(): pl.pallas_call(aggregate_kernel, out_shape=jax.ShapeDtypeStruct((peers, f...  7.05 us
    ppermute x3, starting transfers between devices, per_device(): weight_grad += lax.ppermute(local_grad, 'mb', pairs).astype(jnp.float32)  5.18 us
    ppermute x3, waiting for transfers between devices, per_device(): weight_grad += lax.ppermute(local_grad, 'mb', pairs).astype(jnp.float32)  2.04 us
    pallas_call x3, Pallas kernels, call_in_vmem(): pl.pallas_call(kernel, out_shape=outputs, in_specs=[in_vmem] * len(operan...  1.91 us
  transfers between devices with their start and end apart: 4, of which 2 were waited for; matrix products, arithmetic and copies ran while one was open for 0% of the time, Pallas kernels for 2%

profile of v8, /device:TPU:0, one launch (start us, length us, event | category | flops | bytes accessed | tf_op | source)
XLA Modules:
  0.0 56.6 jit_solution(12062909398953724152)
XLA Ops:
  0.6 0.0 copy-start.1
  0.6 0.0 copy-start
  0.7 7.0 %aggregate.1 = bf16[32,32,512]{2,1,0:T(8,128)(2,1)S(1)} custom-call(s32[192]{0:T(256)} %row_index.1, s32[192]{0:T(256)} %col_index.1, f32[32,65536]{1,0:T(8,128)} %features.1, s32[192,128,128]{2,1,0:T(8,128)} %masks.1), custom_call_target="tpu_custom_call" | custom-call | tf_op jit(solution)/shard_map/aggregate/pallas_call | solution.py:127
  7.7 25.3 %all_to_all.10 = bf16[32,32,512]{2,1,0:T(8,128)(2,1)S(1)} all-to-all(bf16[32,32,512]{2,1,0:T(8,128)(2,1)S(1)} %aggregate.1), channel_id=1, replica_groups=mesh['mb'=4,'z'=4,'x'=4,'core'=2] {'z','x','core'}, dimensions={0} | all-to-all | bytes 2097152 | tf_op jit(solution)/shard_map/all_to_all | solution.py:231
  33.0 0.0 copy-done.1
  33.0 0.0 copy-done
  33.0 0.8 %slopes.1 = (f32[512,256]{1,0:T(8,128)S(1)}, bf16[512,256]{1,0:T(8,128)(2,1)S(1)}, bf16[16,32,256]{2,1,0:T(8,128)(2,1)S(1)}) custom-call(bf16[16,2,32,512]{3,2,1,0:T(8,128)(2,1)S(1)} %bitcast.1, bf16[1024,256]{1,0:T(8,128)(2,1)S(1)} %copy-done, bf16[512,256]{1,0:T(8,128)(2,1)S(1)} %copy-done.1), custom_call_target="tpu_custom_call" | custom-call | tf_op jit(solution)/shard_map/slopes/pallas_call | solution.py:196
  33.8 0.2 collective-permute-start
  34.0 0.3 kept.1
  34.3 1.1 %collective-permute-done = bf16[16,32,256]{2,1,0:T(8,128)(2,1)S(1)} collective-permute-done((bf16[16,32,256]{2,1,0:T(8,128)(2,1)S(1)}, bf16[16,32,256]{2,1,0:T(8,128)(2,1)S(1)}, u32[]{:S(2)}, u32[]{:S(2)}) %collective-permute-start) | collective-permute-done | bytes 262176 | tf_op jit(solution)/shard_map/ppermute | solution.py:221
  35.4 0.1 add_convert_fusion
  35.5 12.4 %all_to_all.11 = bf16[16,32,256]{2,1,0:T(8,128)(2,1)S(1)} all-to-all(bf16[16,32,256]{2,1,0:T(8,128)(2,1)S(1)} %add_convert_fusion), channel_id=1, replica_groups=mesh['mb'=4,'z'=4,'x'=4,'core'=2] {'z','x'}, dimensions={0} | all-to-all | bytes 524288 | tf_op jit(solution)/shard_map/all_to_all | solution.py:234
  48.0 3.1 %collective-permute-start.3 = (bf16[32,256]{1,0:T(8,128)(2,1)S(1)}, bf16[32,256]{1,0:T(8,128)(2,1)S(1)}, u32[]{:S(2)}, u32[]{:S(2)}) collective-permute-start(bf16[32,256]{1,0:T(8,128)(2,1)S(1)} %convert_element_type.24), channel_id=1, source_target_pairs={{0,96},{32,64},{64,0},{96,32},{1,97},{33,65},{65,1},{97,33},{2,98}... | collective-permute-start | bytes 49160 | tf_op jit(solution)/shard_map/ppermute | solution.py:247
  51.1 0.5 collective-permute-start.2
  51.6 1.6 %collective-permute-start.1 = (bf16[32,256]{1,0:T(8,128)(2,1)S(1)}, bf16[32,256]{1,0:T(8,128)(2,1)S(1)}, u32[]{:S(2)}, u32[]{:S(2)}) collective-permute-start(bf16[32,256]{1,0:T(8,128)(2,1)S(1)} %convert_element_type.24), channel_id=1, source_target_pairs={{0,32},{32,0},{64,96},{96,64},{1,33},{33,1},{65,97},{97,65},{2,34}... | collective-permute-start | bytes 49160 | tf_op jit(solution)/shard_map/ppermute | solution.py:247
  53.2 0.8 %activation.1 = bf16[512,256]{1,0:T(8,128)(2,1)} custom-call(f32[512,256]{1,0:T(8,128)S(1)} %get-tuple-element.10.preact), custom_call_target="tpu_custom_call" | custom-call | tf_op jit(solution)/shard_map/activation/pallas_call | solution.py:196
  54.0 0.0 collective-permute-done.3
  54.0 2.0 %collective-permute-done.2 = bf16[32,256]{1,0:T(8,128)(2,1)S(1)} collective-permute-done((bf16[32,256]{1,0:T(8,128)(2,1)S(1)}, bf16[32,256]{1,0:T(8,128)(2,1)S(1)}, u32[]{:S(2)}, u32[]{:S(2)}) %collective-permute-start.2) | collective-permute-done | bytes 16416 | tf_op jit(solution)/shard_map/ppermute | solution.py:247
  56.0 0.0 collective-permute-done.1
  56.0 0.6 %convert_add_fusion = f32[32,256]{1,0:T(8,128)} fusion(bf16[32,256]{1,0:T(8,128)(2,1)S(1)} %collective-permute-done.3, bf16[32,256]{1,0:T(8,128)(2,1)S(1)} %collective-permute-done.2, f32[32,256]{1,0:T(8,128)S(1)} %convert_reduce_fusion, bf16[32,256]{1,0:T(8,128)(2,1)S(1)} %collective-permute-done.1), kind=kLoop, calls=%fused_computation.2 | loop fusion | flops 49152 | bytes 114688 | tf_op jit(solution)/shard_map/add | solution.py:247
  (2 shorter events, 0.0 us)
Async XLA Ops:
  0.6 32.4 %copy-start.1 = (bf16[512,256]{1,0:T(8,128)(2,1)S(1)}, bf16[512,256]{1,0:T(8,128)(2,1)}, u32[]{:S(2)}) copy-start(bf16[512,256]{1,0:T(8,128)(2,1)} %upstream.1) | copy-start | bytes 786436
  0.6 32.4 %copy-start = (bf16[1024,256]{1,0:T(8,128)(2,1)S(1)}, bf16[1024,256]{1,0:T(8,128)(2,1)}, u32[]{:S(2)}) copy-start(bf16[1024,256]{1,0:T(8,128)(2,1)} %weight.1) | copy-start | bytes 1572868
  33.8 1.6 %collective-permute-start = (bf16[16,32,256]{2,1,0:T(8,128)(2,1)S(1)}, bf16[16,32,256]{2,1,0:T(8,128)(2,1)S(1)}, u32[]{:S(2)}, u32[]{:S(2)}) collective-permute-start(bf16[16,32,256]{2,1,0:T(8,128)(2,1)S(1)} %get-tuple-element.8), channel_id=1, source_target_pairs={{0,1},{1,0},{2,3},{3,2},{4,5},{5,4},{6,7},{7,6},{8,9},{9,8},{10,11... | collective-permute-start | bytes 786440 | tf_op jit(solution)/shard_map/ppermute | solution.py:221
  48.0 6.0 %collective-permute-start.3 = (bf16[32,256]{1,0:T(8,128)(2,1)S(1)}, bf16[32,256]{1,0:T(8,128)(2,1)S(1)}, u32[]{:S(2)}, u32[]{:S(2)}) collective-permute-start(bf16[32,256]{1,0:T(8,128)(2,1)S(1)} %convert_element_type.24), channel_id=1, source_target_pairs={{0,96},{32,64},{64,0},{96,32},{1,97},{33,65},{65,1},{97,33},{2,98}... | collective-permute-start | bytes 49160 | tf_op jit(solution)/shard_map/ppermute | solution.py:247
  51.1 4.9 %collective-permute-start.2 = (bf16[32,256]{1,0:T(8,128)(2,1)S(1)}, bf16[32,256]{1,0:T(8,128)(2,1)S(1)}, u32[]{:S(2)}, u32[]{:S(2)}) collective-permute-start(bf16[32,256]{1,0:T(8,128)(2,1)S(1)} %convert_element_type.24), channel_id=1, source_target_pairs={{0,64},{32,96},{64,32},{96,0},{1,65},{33,97},{65,33},{97,1},{2,66}... | collective-permute-start | bytes 49160 | tf_op jit(solution)/shard_map/ppermute | solution.py:247
  51.6 4.4 %collective-permute-start.1 = (bf16[32,256]{1,0:T(8,128)(2,1)S(1)}, bf16[32,256]{1,0:T(8,128)(2,1)S(1)}, u32[]{:S(2)}, u32[]{:S(2)}) collective-permute-start(bf16[32,256]{1,0:T(8,128)(2,1)S(1)} %convert_element_type.24), channel_id=1, source_target_pairs={{0,32},{32,0},{64,96},{96,64},{1,33},{33,1},{65,97},{97,65},{2,34}... | collective-permute-start | bytes 49160 | tf_op jit(solution)/shard_map/ppermute | solution.py:247
